TPU v7x, 256 devices: a whole 4x4x8 slice. The times are simulated.
256 devices in a mesh: grp: 32 (over x_lo, z, core), blk: 8 (over x_hi, y).
Axes of the slice: x: 4 (x_hi: 2, x_lo: 2; x = x_hi * 2 + x_lo), y: 4, z: 8, core: 2. Of those that a mesh axis runs over, the one named last changes fastest.
Arguments:
- walker_matrix: float32 [32, 8, 1024, 1024], P('grp', 'blk'), may hold values from -6 to 6
- updates: bfloat16 [32, 8, 4, 1024, 256], P('grp', 'blk'), may hold values from -0.19921875 to 0.19921875
- update_rows: int32 [32, 8, 4, 256], P('grp', 'blk'), may hold values from 0 to 1023, as said below
- left_table: float32 [1024, 256], replicated, may hold values from -0.1875 to 0.1875
- right_table: float32 [1024, 256], replicated, may hold values from -0.1875 to 0.1875
- assignment: int32 [8, 32], P('blk'), may hold values from 0 to 31, each once within a row
- momentum_sum: int32 [16, 16], replicated, may hold values from 0 to 15, as said below
- transfer_momentum: int32 [32], replicated, may hold values from 0 to 15
- transfer_frequency: int32 [32], replicated, may hold values from 0 to 15
- ownership: int32 [32], P('blk'), may hold values from 0 to 31, each once
- g4_prior: float32 [32, 32, 256, 256], P('grp', 'blk'), may hold values from -6 to 6
Outputs:
- g4_slices: float32 [32, 32, 256, 256], P('grp', 'blk')
Inputs may be any that keep to these rules, and one draw needn't show every extreme that they name: `update_rows`: within each update of each walker the 256 row indices are distinct. `assignment`: each row is a permutation of the grp indices. `momentum_sum`: the addition table of a periodic 4 x 4 cluster under a relabeling of its momenta; every row and column is a permutation. `ownership`: a permutation of the transfer slots.
All inputs are finite; a program needn't handle non-finite values.
Results may differ from a plain program's by a relative error of at most 0.0003.
Values sent between devices are 32-bit elements; how exact they have to be, the bound alone decides.
No kernel may reach another device: no remote copies, remote signals or barrier semaphores. Data moves between devices by JAX's collectives and lax.ppermute only.
A program may use at most 128 MiB of HBM per device.

v0:
```python
import functools

import jax
import jax.numpy as jnp
from jax import lax
from jax.experimental import pallas as pl
from jax.experimental.pallas import tpu as pltpu
from jax.sharding import PartitionSpec as P

UPD = 4
RANK = 256
ORDER = 1024
NW = 16
NK = 16
KW = 256
M_CHUNKS = 8
F32 = jnp.float32
BF16 = jnp.bfloat16

ANY = pl.BlockSpec(memory_space=pl.ANY)
VMEM = pl.BlockSpec(memory_space=pltpu.VMEM)
SMEM = pl.BlockSpec(memory_space=pltpu.SMEM)


def split(x):
    hi = x.astype(BF16)
    return hi, (x - hi.astype(F32)).astype(BF16)


def mm(a, b):
    return jnp.dot(a, b, preferred_element_type=F32)


def mm_nt(a, b):
    return lax.dot_general(a, b, (((1,), (1,)), ((), ())), preferred_element_type=F32)


def walker_kernel(m_hbm, u_hbm, rows_ref, l_hbm, r_hbm, out_ref, m_v, u_v, l_v, r_v, w_ref, t_ref, sems):
    size = ORDER // M_CHUNKS
    copy_l = pltpu.make_async_copy(l_hbm, l_v, sems.at[0])
    copy_r = pltpu.make_async_copy(r_hbm, r_v, sems.at[1])
    copy_u = [pltpu.make_async_copy(u_hbm.at[u], u_v.at[u], sems.at[2 + u]) for u in range(UPD)]
    copy_m = [
        pltpu.make_async_copy(
            m_hbm.at[pl.ds(k * size, size), :], m_v.at[pl.ds(k * size, size), :], sems.at[2 + UPD + k]
        )
        for k in range(M_CHUNKS)
    ]
    copy_l.start()
    for u in reversed(range(UPD)):
        copy_u[u].start()
    for copy in copy_m:
        copy.start()
    copy_r.start()

    lane = lax.broadcasted_iota(jnp.int32, (RANK, ORDER), 1)
    copy_l.wait()
    w_ref[...] = l_v[...].T
    for u in reversed(range(UPD)):
        column = jnp.broadcast_to(rows_ref[pl.ds(u, 1), :], (128, RANK)).T[:, :1]
        chosen = jnp.where(lane == column, 1.0, 0.0).astype(BF16)
        w_hi, w_lo = split(w_ref[...])
        copy_u[u].wait()
        x = mm(w_hi, u_v[u]) + mm(w_lo, u_v[u])
        x_hi, x_lo = split(x)
        w_ref[...] += mm(x_hi, chosen) + mm(x_lo, chosen)
    w_hi, w_lo = split(w_ref[...])
    for k in range(M_CHUNKS):
        copy_m[k].wait()
        m_hi, m_lo = split(m_v[pl.ds(k * size, size), :])
        part_hi = w_hi[:, k * size : (k + 1) * size]
        part_lo = w_lo[:, k * size : (k + 1) * size]
        term = mm(part_hi, m_hi) + mm(part_lo, m_hi) + mm(part_hi, m_lo)
        if k == 0:
            t_ref[...] = term
        else:
            t_ref[...] += term
    copy_r.wait()
    t_hi, t_lo = split(t_ref[...])
    r_hi, r_lo = split(r_v[...])
    out_ref[...] = mm(t_hi, r_hi) + mm(t_lo, r_hi) + mm(t_hi, r_lo)


def walker(matrix, updates, rows, left, right):
    return pl.pallas_call(
        walker_kernel,
        out_shape=jax.ShapeDtypeStruct((KW, KW), F32),
        in_specs=[ANY, ANY, VMEM, ANY, ANY],
        out_specs=VMEM,
        scratch_shapes=[
            pltpu.VMEM((ORDER, ORDER), F32),
            pltpu.VMEM((UPD, ORDER, RANK), BF16),
            pltpu.VMEM((ORDER, KW), F32),
            pltpu.VMEM((ORDER, KW), F32),
            pltpu.VMEM((KW, ORDER), F32),
            pltpu.VMEM((KW, ORDER), F32),
            pltpu.SemaphoreType.DMA((2 + UPD + M_CHUNKS,)),
        ],
        compiler_params=pltpu.CompilerParams(vmem_limit_bytes=40 << 20),
        name="walker",
    )(matrix, updates, rows, left, right)


def route_kernel(n, targets_ref, x_ref, out_ref):
    for w in range(n):
        out_ref[targets_ref[0, w]] = x_ref[w]


def route(targets, chunks):
    return pl.pallas_call(
        functools.partial(route_kernel, chunks.shape[0]),
        out_shape=jax.ShapeDtypeStruct(chunks.shape, F32),
        in_specs=[SMEM, VMEM],
        out_specs=VMEM,
        name="route",
    )(targets, chunks)


def tail_kernel(
    scale, own_ref, ms_ref, tm_ref, tf_ref, two_ref, up_ref, down_ref, far_a_ref, far_b_ref, prior_ref, out_ref,
    pi_ref, a_ref, v_hi, v_lo,
):
    held = own_ref.shape[0]
    lanes = lax.broadcasted_iota(jnp.int32, (NW, KW), 1)
    steps = lax.broadcasted_iota(jnp.int32, (NW, KW), 0)
    for j in range(held):
        label = own_ref[j]
        moment = tm_ref[label]
        spot = (steps + tf_ref[label]) % NW
        for kappa in range(NK):
            goal = spot + ms_ref[kappa, moment] * NW
            pi_ref[pl.ds(j * KW + kappa * NW, NW), :] = jnp.where(lanes == goal, 1.0, 0.0).astype(BF16)
    half = KW // 2
    for p in range(2):
        a_ref[p] = two_ref[p]
        a_ref[2 + p] = up_ref[p]
        a_ref[4 + p] = down_ref[p]
        a_ref[6 + p, pl.ds(0, half), :] = far_a_ref[p]
        a_ref[6 + p, pl.ds(half, half), :] = far_b_ref[p]
    pi = pi_ref[...]
    for b in range(8):
        a_hi, a_lo = split(a_ref[b])
        h = mm_nt(pi, a_hi).astype(BF16)
        l = mm_nt(pi, a_lo).astype(BF16)
        for j in range(held):
            v_hi[j, pl.ds(b * KW, KW), :] = h[j * KW : (j + 1) * KW]
            v_lo[j, pl.ds(b * KW, KW), :] = l[j * KW : (j + 1) * KW]
    for j in range(held):
        pi_j = pi_ref[pl.ds(j * KW, KW), :]
        total = None
        for b in range(8):
            rows = pl.ds(b * KW, KW)
            z = mm_nt(v_hi[j, rows, :], pi_j) + mm_nt(v_lo[j, rows, :], pi_j)
            term = a_ref[b] * z
            total = term if total is None else total + term
        out_ref[j] = prior_ref[j] + total * scale


def tail(scale, ownership, momentum_sum, moments, freqs, pieces, prior):
    held = ownership.shape[0]
    return pl.pallas_call(
        functools.partial(tail_kernel, scale),
        out_shape=jax.ShapeDtypeStruct(prior.shape, F32),
        in_specs=[SMEM] * 4 + [VMEM] * 6,
        out_specs=VMEM,
        scratch_shapes=[
            pltpu.VMEM((held * KW, KW), BF16),
            pltpu.VMEM((8, KW, KW), F32),
            pltpu.VMEM((held, 8 * KW, KW), BF16),
            pltpu.VMEM((held, 8 * KW, KW), BF16),
        ],
        compiler_params=pltpu.CompilerParams(vmem_limit_bytes=48 << 20),
        name="tail",
    )(ownership, momentum_sum, moments, freqs, *pieces, prior)


def gather_cycle(own):
    half = KW // 2
    across = [(j, (j + 4) % 8) for j in range(8)]
    upward = [(j, j // 4 * 4 + (j % 4 + 1) % 4) for j in range(8)]
    downward = [(j, j // 4 * 4 + (j % 4 + 3) % 4) for j in range(8)]
    two = jnp.stack([own, lax.ppermute(own, "blk", across)])
    up = lax.ppermute(two, "blk", upward)
    down = lax.ppermute(two, "blk", downward)
    far_a = lax.ppermute(up[:, :half], "blk", upward)
    far_b = lax.ppermute(down[:, half:], "blk", downward)
    return two, up, down, far_a, far_b


def shards(
    walker_matrix, updates, update_rows, left_table, right_table, assignment, momentum_sum,
    transfer_momentum, transfer_frequency, ownership, g4_prior,
):
    n_grp = lax.axis_size("grp")
    greens = walker(walker_matrix[0, 0], updates[0, 0], update_rows[0, 0], left_table, right_table)
    chunks = lax.all_to_all(greens.reshape(n_grp, KW // n_grp, KW), "grp", 0, 0, tiled=True)
    routed = route(assignment, chunks)
    measured = lax.all_to_all(routed, "grp", 0, 0, tiled=True).reshape(KW, KW)
    pieces = gather_cycle(measured)
    scale = 1.0 / lax.axis_size("blk")
    return tail(scale, ownership, momentum_sum, transfer_momentum, transfer_frequency, pieces, g4_prior[0])[None]


def solution(mesh):
    placed = (
        P("grp", "blk", None, None),
        P("grp", "blk", None, None, None),
        P("grp", "blk", None, None),
        P(),
        P(),
        P("blk", None),
        P(),
        P(),
        P(),
        P("blk"),
        P("grp", "blk", None, None),
    )
    return jax.shard_map(
        shards, mesh=mesh, in_specs=placed, out_specs=P("grp", "blk", None, None), check_vma=False
    )
```

profile of v0, /device:TPU:32, one launch (start us, length us, event | category | flops | bytes accessed | tf_op | source)
XLA Modules:
  0.0 98.0 jit_solution(6739526438003570606)
XLA Ops:
  0.0 2.2 %copy-done = f32[1,1,1024,1024]{3,2,1,0:T(8,128)S(1)} copy-done((f32[1,1,1024,1024]{3,2,1,0:T(8,128)S(1)}, f32[1,1,1024,1024]{3,2,1,0:T(8,128)}, u32[]{:S(2)}) %copy-start) | copy-done | bytes 4194328
  2.2 1.6 %copy-done.1 = bf16[1,1,4,1024,256]{4,3,2,1,0:T(8,128)(2,1)S(1)} copy-done((bf16[1,1,4,1024,256]{4,3,2,1,0:T(8,128)(2,1)S(1)}, bf16[1,1,4,1024,256]{4,3,2,1,0:T(8,128)(2,1)}, u32[]{:S(2)}) %copy-start.1) | copy-done | bytes 2097176
  3.8 1.2 %copy-done.3 = f32[1024,256]{1,0:T(8,128)S(1)} copy-done((f32[1024,256]{1,0:T(8,128)S(1)}, f32[1024,256]{1,0:T(8,128)}, u32[]{:S(2)}) %copy-start.3) | copy-done | bytes 1048600
  5.0 1.2 %copy-done.4 = f32[1024,256]{1,0:T(8,128)S(1)} copy-done((f32[1024,256]{1,0:T(8,128)S(1)}, f32[1024,256]{1,0:T(8,128)}, u32[]{:S(2)}) %copy-start.4) | copy-done | bytes 1048600
  6.2 0.7 copy-done.6
  6.9 0.0 copy-start.9
  6.9 11.1 %walker.1 = f32[256,256]{1,0:T(8,128)S(1)} custom-call(f32[1024,1024]{1,0:T(8,128)S(1)} %bitcast.9, bf16[4,1024,256]{2,1,0:T(8,128)(2,1)S(1)} %bitcast.10, s32[4,256]{1,0:T(4,128)S(1)} %bitcast.13, f32[1024,256]{1,0:T(8,128)S(1)} %copy-done.3, f32[1024,256]{1,0:T(8,128)S(1)} %copy-done.4), custom_call_target="tpu_custom_call" | custom-call | tf_op jit(solution)/shard_map/walker/pallas_call | solution.py:85
  18.0 21.7 %all_to_all.10.x_ref = f32[32,8,256]{2,1,0:T(8,128)} all-to-all(f32[32,8,256]{2,1,0:T(8,128)S(1)} %bitcast.12), channel_id=1, replica_groups=mesh['grp'=32,'blk'=8] {'grp'}, dimensions={0} | all-to-all | bytes 524288 | tf_op jit(solution)/shard_map/all_to_all | solution.py:196
  39.7 1.7 %route.1 = f32[32,8,256]{2,1,0:T(8,128)} custom-call(s32[1,32]{1,0:T(1,128)} %targets_ref.1, f32[32,8,256]{2,1,0:T(8,128)} %all_to_all.10.x_ref), custom_call_target="tpu_custom_call" | custom-call | tf_op jit(solution)/shard_map/route/pallas_call | solution.py:110
  41.4 17.0 %all_to_all.11 = f32[32,8,256]{2,1,0:T(8,128)S(1)} all-to-all(f32[32,8,256]{2,1,0:T(8,128)} %route.1), channel_id=1, replica_groups=mesh['grp'=32,'blk'=8] {'grp'}, dimensions={0} | all-to-all | bytes 524288 | tf_op jit(solution)/shard_map/all_to_all | solution.py:198
  58.4 2.7 %collective-permute-start = (f32[256,256]{1,0:T(8,128)S(1)}, f32[256,256]{1,0:T(8,128)S(1)}, u32[]{:S(2)}, u32[]{:S(2)}) collective-permute-start(f32[256,256]{1,0:T(8,128)S(1)} %bitcast.14), channel_id=1, source_target_pairs={{0,4},{1,5},{2,6},{3,7},{4,0},{5,1},{6,2},{7,3},{8,12},{9,13},{10,... | collective-permute-start | bytes 786440 | tf_op jit(solution)/shard_map/ppermute | solution.py:182
  61.2 6.0 %collective-permute-done = f32[256,256]{1,0:T(8,128)S(1)} collective-permute-done((f32[256,256]{1,0:T(8,128)S(1)}, f32[256,256]{1,0:T(8,128)S(1)}, u32[]{:S(2)}, u32[]{:S(2)}) %collective-permute-start) | collective-permute-done | bytes 262176 | tf_op jit(solution)/shard_map/ppermute | solution.py:182
  67.2 3.1 %collective-permute-start.2 = (f32[2,256,256]{2,1,0:T(8,128)S(1)}, f32[2,256,256]{2,1,0:T(8,128)S(1)}, u32[]{:S(2)}, u32[]{:S(2)}) collective-permute-start(f32[2,256,256]{2,1,0:T(8,128)S(1)} %pad_maximum_fusion.two_ref), channel_id=1, source_target_pairs={{0,3},{1,0},{2,1},{3,2},{4,7},{5,4},{6,5},{7,6},{8,11},{9,8},{10,9... | collective-permute-start | bytes 1572872 | tf_op jit(solution)/shard_map/ppermute | solution.py:184
  70.3 0.0 collective-permute-start.1
  70.3 9.5 %collective-permute-done.2.down_ref = f32[2,256,256]{2,1,0:T(8,128)S(1)} collective-permute-done((f32[2,256,256]{2,1,0:T(8,128)S(1)}, f32[2,256,256]{2,1,0:T(8,128)S(1)}, u32[]{:S(2)}, u32[]{:S(2)}) %collective-permute-start.2) | collective-permute-done | bytes 524320 | tf_op jit(solution)/shard_map/ppermute | solution.py:184
  79.8 3.8 %collective-permute-start.4 = (f32[2,128,256]{2,1,0:T(8,128)S(1)}, f32[2,128,256]{2,1,0:T(8,128)S(1)}, u32[]{:S(2)}, u32[]{:S(2)}) collective-permute-start(f32[2,128,256]{2,1,0:T(8,128)S(1)} %slice.9), channel_id=1, source_target_pairs={{0,3},{1,0},{2,1},{3,2},{4,7},{5,4},{6,5},{7,6},{8,11},{9,8},{10,9... | collective-permute-start | bytes 786440 | tf_op jit(solution)/shard_map/ppermute | solution.py:186
  83.6 0.0 collective-permute-done.1.up_ref
  83.6 0.3 collective-permute-start.3
  83.9 3.6 %collective-permute-done.4.far_b_ref = f32[2,128,256]{2,1,0:T(8,128)S(1)} collective-permute-done((f32[2,128,256]{2,1,0:T(8,128)S(1)}, f32[2,128,256]{2,1,0:T(8,128)S(1)}, u32[]{:S(2)}, u32[]{:S(2)}) %collective-permute-start.4) | collective-permute-done | bytes 262176 | tf_op jit(solution)/shard_map/ppermute | solution.py:186
  87.5 4.0 %collective-permute-done.3.far_a_ref = f32[2,128,256]{2,1,0:T(8,128)S(1)} collective-permute-done((f32[2,128,256]{2,1,0:T(8,128)S(1)}, f32[2,128,256]{2,1,0:T(8,128)S(1)}, u32[]{:S(2)}, u32[]{:S(2)}) %collective-permute-start.3) | collective-permute-done | bytes 262176 | tf_op jit(solution)/shard_map/ppermute | solution.py:185
  91.5 0.0 copy-done.7
  91.5 0.0 copy-done.8
  91.5 0.0 copy-done.9
  91.5 6.5 %tail.1 = f32[4,256,256]{2,1,0:T(8,128)} custom-call(s32[4]{0:T(128)S(1)} %copy-done.7, s32[16,16]{1,0:T(8,128)S(1)} %copy-done.5, s32[32]{0:T(128)S(1)} %copy-done.8, s32[32]{0:T(128)S(1)} %copy-done.9, f32[2,256,256]{2,1,0:T(8,128)S(1)} %pad_maximum_fusion.two_ref, f32[2,256,256]{2,1,0:T(8,128)S(1)} %collective-permute-done.1.up_ref, ...), custom_call_target="tpu_custom_call" | custom-call | tf_op jit(solution)/shard_map/tail/pallas_call | solution.py:161
  (14 shorter events, 0.1 us)
Async XLA Ops:
  0.0 2.2 %copy-start = (f32[1,1,1024,1024]{3,2,1,0:T(8,128)S(1)}, f32[1,1,1024,1024]{3,2,1,0:T(8,128)}, u32[]{:S(2)}) copy-start(f32[1,1,1024,1024]{3,2,1,0:T(8,128)} %param.11) | copy-start | bytes 12582916
  2.2 1.6 %copy-start.1 = (bf16[1,1,4,1024,256]{4,3,2,1,0:T(8,128)(2,1)S(1)}, bf16[1,1,4,1024,256]{4,3,2,1,0:T(8,128)(2,1)}, u32[]{:S(2)}) copy-start(bf16[1,1,4,1024,256]{4,3,2,1,0:T(8,128)(2,1)} %param.12) | copy-start | bytes 6291460
  3.8 1.2 %copy-start.3 = (f32[1024,256]{1,0:T(8,128)S(1)}, f32[1024,256]{1,0:T(8,128)}, u32[]{:S(2)}) copy-start(f32[1024,256]{1,0:T(8,128)} %l_hbm.1) | copy-start | bytes 3145732
  5.0 1.2 %copy-start.4 = (f32[1024,256]{1,0:T(8,128)S(1)}, f32[1024,256]{1,0:T(8,128)}, u32[]{:S(2)}) copy-start(f32[1024,256]{1,0:T(8,128)} %r_hbm.1) | copy-start | bytes 3145732
  6.2 0.7 copy-start.6
  6.9 84.6 %copy-start.2 = (f32[1,4,256,256]{3,2,1,0:T(8,128)S(1)}, f32[1,4,256,256]{3,2,1,0:T(8,128)}, u32[]{:S(2)}) copy-start(f32[1,4,256,256]{3,2,1,0:T(8,128)} %param.21) | copy-start | bytes 3145732
  6.9 84.6 %copy-start.5 = (s32[16,16]{1,0:T(8,128)S(1)}, s32[16,16]{1,0:T(8,128)}, u32[]{:S(2)}) copy-start(s32[16,16]{1,0:T(8,128)} %ms_ref.1) | copy-start | bytes 3076
  6.9 84.6 %copy-start.7 = (s32[4]{0:T(128)S(1)}, s32[4]{0:T(128)}, u32[]{:S(2)}) copy-start(s32[4]{0:T(128)} %own_ref.1) | copy-start | bytes 52
  6.9 84.6 %copy-start.8 = (s32[32]{0:T(128)S(1)}, s32[32]{0:T(128)}, u32[]{:S(2)}) copy-start(s32[32]{0:T(128)} %tm_ref.1) | copy-start | bytes 388
  6.9 84.6 %copy-start.9 = (s32[32]{0:T(128)S(1)}, s32[32]{0:T(128)}, u32[]{:S(2)}) copy-start(s32[32]{0:T(128)} %tf_ref.1) | copy-start | bytes 388
  58.4 8.8 %collective-permute-start = (f32[256,256]{1,0:T(8,128)S(1)}, f32[256,256]{1,0:T(8,128)S(1)}, u32[]{:S(2)}, u32[]{:S(2)}) collective-permute-start(f32[256,256]{1,0:T(8,128)S(1)} %bitcast.14), channel_id=1, source_target_pairs={{0,4},{1,5},{2,6},{3,7},{4,0},{5,1},{6,2},{7,3},{8,12},{9,13},{10,... | collective-permute-start | bytes 786440 | tf_op jit(solution)/shard_map/ppermute | solution.py:182
  67.2 12.6 %collective-permute-start.2 = (f32[2,256,256]{2,1,0:T(8,128)S(1)}, f32[2,256,256]{2,1,0:T(8,128)S(1)}, u32[]{:S(2)}, u32[]{:S(2)}) collective-permute-start(f32[2,256,256]{2,1,0:T(8,128)S(1)} %pad_maximum_fusion.two_ref), channel_id=1, source_target_pairs={{0,3},{1,0},{2,1},{3,2},{4,7},{5,4},{6,5},{7,6},{8,11},{9,8},{10,9... | collective-permute-start | bytes 1572872 | tf_op jit(solution)/shard_map/ppermute | solution.py:184
  70.3 13.3 %collective-permute-start.1 = (f32[2,256,256]{2,1,0:T(8,128)S(1)}, f32[2,256,256]{2,1,0:T(8,128)S(1)}, u32[]{:S(2)}, u32[]{:S(2)}) collective-permute-start(f32[2,256,256]{2,1,0:T(8,128)S(1)} %pad_maximum_fusion.two_ref), channel_id=1, source_target_pairs={{0,1},{1,2},{2,3},{3,0},{4,5},{5,6},{6,7},{7,4},{8,9},{9,10},{10,1... | collective-permute-start | bytes 1572872 | tf_op jit(solution)/shard_map/ppermute | solution.py:183
  79.8 7.7 %collective-permute-start.4 = (f32[2,128,256]{2,1,0:T(8,128)S(1)}, f32[2,128,256]{2,1,0:T(8,128)S(1)}, u32[]{:S(2)}, u32[]{:S(2)}) collective-permute-start(f32[2,128,256]{2,1,0:T(8,128)S(1)} %slice.9), channel_id=1, source_target_pairs={{0,3},{1,0},{2,1},{3,2},{4,7},{5,4},{6,5},{7,6},{8,11},{9,8},{10,9... | collective-permute-start | bytes 786440 | tf_op jit(solution)/shard_map/ppermute | solution.py:186
  83.6 7.8 %collective-permute-start.3 = (f32[2,128,256]{2,1,0:T(8,128)S(1)}, f32[2,128,256]{2,1,0:T(8,128)S(1)}, u32[]{:S(2)}, u32[]{:S(2)}) collective-permute-start(f32[2,128,256]{2,1,0:T(8,128)S(1)} %slice.8), channel_id=1, source_target_pairs={{0,1},{1,2},{2,3},{3,0},{4,5},{5,6},{6,7},{7,4},{8,9},{9,10},{10,1... | collective-permute-start | bytes 786440 | tf_op jit(solution)/shard_map/ppermute | solution.py:185
where the time goes:
time: 99.2 us; the launch traced here: 98 us
  blocking collectives  38.7 us (39%)
  waiting for transfers between devices  23.1 us (23%)
  Pallas kernels  19.3 us (19%)
  starting transfers between devices  9.84 us (10%)
  local copies, waits for them, and re-layouts  6.97 us (7%)
    all_to_all x1, blocking collectives, shards(): lax.all_to_all(greens.reshape(n_grp, KW // n_grp, KW), 'grp', 0, 0, tiled...  21.7 us
    all_to_all x1, blocking collectives, shards(): measured = lax.all_to_all(routed, 'grp', 0, 0, tiled=True).reshape(KW, KW)  17 us
    pallas_call x1, Pallas kernels, walker(): pl.pallas_call(walker_kernel, out_shape=jax.ShapeDtypeStruct((KW, KW), F3...  11.1 us
    ppermute x1, waiting for transfers between devices, gather_cycle(): down = lax.ppermute(two, 'blk', downward)  9.47 us
    unnamed x20, local copies, waits for them, and re-layouts  6.93 us
    pallas_call x1, Pallas kernels, tail(): pl.pallas_call(functools.partial(tail_kernel, scale), out_shape=jax.Shape...  6.53 us
    ppermute x1, waiting for transfers between devices, gather_cycle(): two = jnp.stack([own, lax.ppermute(own, 'blk', across)])  6.05 us
    ppermute x1, waiting for transfers between devices, gather_cycle(): far_a = lax.ppermute(up[:, :half], 'blk', upward)  3.97 us
  transfers between devices with their start and end apart: 5, of which 4 were waited for; matrix products, arithmetic and copies ran while one was open for 0% of the time, Pallas kernels for 0%

commit v1 on v0

v1 whole, which is shorter than its diff:
```python
import functools

import jax
import jax.numpy as jnp
from jax import lax
from jax.experimental import pallas as pl
from jax.experimental.pallas import tpu as pltpu
from jax.sharding import PartitionSpec as P

UPD = 4
RANK = 256
ORDER = 1024
NW = 16
NK = 16
KW = 256
M_CHUNKS = 8
F32 = jnp.float32
BF16 = jnp.bfloat16

HBM = pl.BlockSpec(memory_space=pltpu.HBM)
VMEM = pl.BlockSpec(memory_space=pltpu.VMEM)
SMEM = pl.BlockSpec(memory_space=pltpu.SMEM)


def split(x):
    hi = x.astype(BF16)
    return hi, (x - hi.astype(F32)).astype(BF16)


def mm(a, b):
    return jnp.dot(a, b, preferred_element_type=F32)


def mm_nt(a, b):
    return lax.dot_general(a, b, (((1,), (1,)), ((), ())), preferred_element_type=F32)


def walker_kernel(m_hbm, u_hbm, rows_hbm, l_hbm, r_hbm, out_ref, m_v, u_v, rows_v, l_v, r_v, w_ref, t_ref, sems):
    size = ORDER // M_CHUNKS
    copy_l = pltpu.make_async_copy(l_hbm, l_v, sems.at[0])
    copy_r = pltpu.make_async_copy(r_hbm, r_v, sems.at[1])
    copy_u = [pltpu.make_async_copy(u_hbm.at[u], u_v.at[u], sems.at[2 + u]) for u in range(UPD)]
    copy_m = [
        pltpu.make_async_copy(
            m_hbm.at[pl.ds(k * size, size), :], m_v.at[pl.ds(k * size, size), :], sems.at[2 + UPD + k]
        )
        for k in range(M_CHUNKS)
    ]
    copy_rows = pltpu.make_async_copy(rows_hbm, rows_v, sems.at[2 + UPD + M_CHUNKS])
    copy_l.start()
    copy_rows.start()
    for u in reversed(range(UPD)):
        copy_u[u].start()
    for copy in copy_m:
        copy.start()
    copy_r.start()

    lane = lax.broadcasted_iota(jnp.int32, (RANK, ORDER), 1)
    copy_l.wait()
    copy_rows.wait()
    w_ref[...] = l_v[...].T
    for u in reversed(range(UPD)):
        column = jnp.broadcast_to(rows_v[pl.ds(u, 1), :], (128, RANK)).T[:, :1]
        chosen = jnp.where(lane == column, 1.0, 0.0).astype(BF16)
        w_hi, w_lo = split(w_ref[...])
        copy_u[u].wait()
        x = mm(w_hi, u_v[u]) + mm(w_lo, u_v[u])
        x_hi, x_lo = split(x)
        w_ref[...] += mm(x_hi, chosen) + mm(x_lo, chosen)
    w_hi, w_lo = split(w_ref[...])
    for k in range(M_CHUNKS):
        copy_m[k].wait()
        m_hi, m_lo = split(m_v[pl.ds(k * size, size), :])
        part_hi = w_hi[:, k * size : (k + 1) * size]
        part_lo = w_lo[:, k * size : (k + 1) * size]
        term = mm(part_hi, m_hi) + mm(part_lo, m_hi) + mm(part_hi, m_lo)
        if k == 0:
            t_ref[...] = term
        else:
            t_ref[...] += term
    copy_r.wait()
    t_hi, t_lo = split(t_ref[...])
    r_hi, r_lo = split(r_v[...])
    out_ref[...] = mm(t_hi, r_hi) + mm(t_lo, r_hi) + mm(t_hi, r_lo)


def walker(matrix, updates, rows, left, right):
    return pl.pallas_call(
        walker_kernel,
        out_shape=jax.ShapeDtypeStruct((KW, KW), F32),
        in_specs=[HBM] * 5,
        out_specs=VMEM,
        scratch_shapes=[
            pltpu.VMEM((ORDER, ORDER), F32),
            pltpu.VMEM((UPD, ORDER, RANK), BF16),
            pltpu.VMEM((UPD, RANK), jnp.int32),
            pltpu.VMEM((ORDER, KW), F32),
            pltpu.VMEM((ORDER, KW), F32),
            pltpu.VMEM((KW, ORDER), F32),
            pltpu.VMEM((KW, ORDER), F32),
            pltpu.SemaphoreType.DMA((3 + UPD + M_CHUNKS,)),
        ],
        compiler_params=pltpu.CompilerParams(vmem_limit_bytes=60 << 20),
        name="walker",
    )(matrix, updates, rows, left, right)


def route_kernel(n, targets_ref, x_ref, out_ref):
    for w in range(n):
        out_ref[targets_ref[0, w]] = x_ref[w]


def route(targets, chunks):
    return pl.pallas_call(
        functools.partial(route_kernel, chunks.shape[0]),
        out_shape=jax.ShapeDtypeStruct(chunks.shape, F32),
        in_specs=[SMEM, VMEM],
        out_specs=VMEM,
        compiler_params=pltpu.CompilerParams(vmem_limit_bytes=8 << 20),
        name="route",
    )(targets, chunks)


def labels_kernel(own_ref, ms_ref, tm_ref, tf_ref, pi_ref):
    lanes = lax.broadcasted_iota(jnp.int32, (NW, KW), 1)
    steps = lax.broadcasted_iota(jnp.int32, (NW, KW), 0)
    for j in range(own_ref.shape[0]):
        label = own_ref[j]
        moment = tm_ref[label]
        spot = (steps + tf_ref[label]) % NW
        for kappa in range(NK):
            goal = spot + ms_ref[kappa, moment] * NW
            pi_ref[pl.ds(j * KW + kappa * NW, NW), :] = jnp.where(lanes == goal, 1.0, 0.0).astype(BF16)


def labels(ownership, momentum_sum, moments, freqs):
    held = ownership.shape[0]
    return pl.pallas_call(
        labels_kernel,
        out_shape=jax.ShapeDtypeStruct((held * KW, KW), BF16),
        in_specs=[SMEM] * 4,
        out_specs=VMEM,
        cost_estimate=pl.CostEstimate(flops=4_000_000, bytes_accessed=1_000_000, transcendentals=0),
        compiler_params=pltpu.CompilerParams(vmem_limit_bytes=8 << 20),
        name="labels",
    )(ownership, momentum_sum, moments, freqs)


def products_kernel(scale, picks, pi_ref, *refs):
    *piece_refs, total_ref, out_ref = refs
    held = total_ref.shape[0]
    pi = pi_ref[...]
    terms = [total_ref[j] for j in range(held)]
    for pick in picks:
        parts = [piece_refs[number][pl.ds(start, count), :] for number, start, count in pick]
        a = parts[0] if len(parts) == 1 else jnp.concatenate(parts, axis=0)
        a_hi, a_lo = split(a)
        v_hi = mm_nt(pi, a_hi).astype(BF16)
        v_lo = mm_nt(pi, a_lo).astype(BF16)
        a = a * scale
        for j in range(held):
            rows = slice(j * KW, (j + 1) * KW)
            terms[j] += a * (mm_nt(v_hi[rows], pi[rows]) + mm_nt(v_lo[rows], pi[rows]))
    for j in range(held):
        out_ref[j] = terms[j]


def products(scale, pi, picks, pieces, total, name):
    held = total.shape[0]
    count = len(picks)
    return pl.pallas_call(
        functools.partial(products_kernel, scale, picks),
        out_shape=jax.ShapeDtypeStruct(total.shape, F32),
        in_specs=[VMEM] * (2 + len(pieces)),
        out_specs=VMEM,
        cost_estimate=pl.CostEstimate(
            flops=count * held * 8 * KW**3, bytes_accessed=4 * KW * KW * (2 * held + count), transcendentals=0
        ),
        compiler_params=pltpu.CompilerParams(vmem_limit_bytes=16 << 20),
        name=name,
    )(pi, *pieces, total)


def cycle_products(scale, pi, own, prior):
    half = KW // 2
    whole = (0, KW)
    across = [(j, (j + 4) % 8) for j in range(8)]
    upward = [(j, j // 4 * 4 + (j % 4 + 1) % 4) for j in range(8)]
    downward = [(j, j // 4 * 4 + (j % 4 + 3) % 4) for j in range(8)]
    below = lax.ppermute(own, "blk", upward)
    above = lax.ppermute(own, "blk", downward)
    beside = lax.ppermute(own, "blk", across)
    total = products(scale, pi, [[(0, *whole)]], [own], prior, "products_own")
    below, above, beside, total = lax.optimization_barrier((below, above, beside, total))
    up = lax.ppermute(jnp.concatenate([beside, below[:half]]), "blk", upward)
    down = lax.ppermute(jnp.concatenate([beside, above[half:]]), "blk", downward)
    total = products(
        scale, pi, [[(number, *whole)] for number in range(3)], [below, above, beside], total, "products_near"
    )
    far_up = lax.ppermute(up[:half], "blk", upward)
    far_down = lax.ppermute(down[half:KW], "blk", downward)
    total = products(
        scale,
        pi,
        [[(0, *whole)], [(1, *whole)], [(0, KW, half), (1, KW, half)]],
        [up, down],
        total,
        "products_beside",
    )
    return products(scale, pi, [[(0, 0, half), (1, 0, half)]], [far_up, far_down], total, "products_far")


def shards(
    walker_matrix, updates, update_rows, left_table, right_table, assignment, momentum_sum,
    transfer_momentum, transfer_frequency, ownership, g4_prior,
):
    n_grp = lax.axis_size("grp")
    pi = labels(ownership, momentum_sum, transfer_momentum, transfer_frequency)
    greens = walker(walker_matrix[0, 0], updates[0, 0], update_rows[0, 0], left_table, right_table)
    chunks = lax.all_to_all(greens.reshape(n_grp, KW // n_grp, KW), "grp", 0, 0, tiled=True)
    routed = route(assignment, chunks)
    measured = lax.all_to_all(routed, "grp", 0, 0, tiled=True).reshape(KW, KW)
    scale = 1.0 / lax.axis_size("blk")
    return cycle_products(scale, pi, measured, g4_prior[0])[None]


def solution(mesh):
    placed = (
        P("grp", "blk", None, None),
        P("grp", "blk", None, None, None),
        P("grp", "blk", None, None),
        P(),
        P(),
        P("blk", None),
        P(),
        P(),
        P(),
        P("blk"),
        P("grp", "blk", None, None),
    )
    return jax.shard_map(
        shards, mesh=mesh, in_specs=placed, out_specs=P("grp", "blk", None, None), check_vma=False
    )
```

time: 99.2 us -> 82.3 us (0.83)
  waiting for transfers between devices: 23.1 us -> 9.51 us
  local copies, waits for them, and re-layouts: 6.97 us -> 0.06 us
  starting transfers between devices: 9.84 us -> 12.7 us
  Pallas kernels: 19.3 us -> 20.3 us
    ppermute x5 -> x7, waiting for transfers between devices: 23.1 us -> 9.51 us  [the longest x1 4.68 us: cycle_products(): up = lax.ppermute(jnp.concatenate([beside, below[:half]]), 'blk', upward)]
    unnamed x20 -> x12, local copies, waits for them, and re-layouts: 6.93 us -> 0.02 us
    ppermute x5 -> x7, starting transfers between devices: 9.84 us -> 12.7 us  [the longest x1 3.29 us: cycle_products(): far_down = lax.ppermute(down[half:KW], 'blk', downward)]
    pallas_call x1, Pallas kernels: 11.1 us -> 12.5 us  [walker(): pl.pallas_call(walker_kernel, out_shape=jax.ShapeDtypeStruct((KW, KW), F3...]
    pallas_call x1, Pallas kernels: 1.69 us -> 0.57 us  [route(): pl.pallas_call(functools.partial(route_kernel, chunks.shape[0]), out_shap...]
    pallas_call x1 -> x5, Pallas kernels: 6.53 us -> 7.17 us  [the longest x4 6.35 us: products(): pl.pallas_call(functools.partial(products_kernel, scale, picks), out_shap...]
  transfers between devices with their start and end apart: 5 -> 7, of which waited for: 4 -> 4; matrix products, arithmetic and copies ran while one was open for 0% -> 0% of each run, Pallas kernels for 0% -> 7%
where the time goes in v1:
time: 82.3 us; the launch traced here: 80.6 us
  blocking collectives  38 us (46%)
  Pallas kernels  20.3 us (25%)
  starting transfers between devices  12.7 us (15%)
  waiting for transfers between devices  9.51 us (12%)
    all_to_all x1, blocking collectives, shards(): lax.all_to_all(greens.reshape(n_grp, KW // n_grp, KW), 'grp', 0, 0, tiled...  21.8 us
    all_to_all x1, blocking collectives, shards(): measured = lax.all_to_all(routed, 'grp', 0, 0, tiled=True).reshape(KW, KW)  16.2 us
    pallas_call x1, Pallas kernels, walker(): pl.pallas_call(walker_kernel, out_shape=jax.ShapeDtypeStruct((KW, KW), F3...  12.5 us
    pallas_call x4, Pallas kernels, products(): pl.pallas_call(functools.partial(products_kernel, scale, picks), out_shap...  6.35 us
    ppermute x1, waiting for transfers between devices, cycle_products(): up = lax.ppermute(jnp.concatenate([beside, below[:half]]), 'blk', upward)  4.68 us
    ppermute x1, starting transfers between devices, cycle_products(): far_down = lax.ppermute(down[half:KW], 'blk', downward)  3.29 us
    ppermute x1, waiting for transfers between devices, cycle_products(): beside = lax.ppermute(own, 'blk', across)  2.95 us
    ppermute x1, starting transfers between devices, cycle_products(): lax.ppermute(jnp.concatenate([beside, above[half:]]), 'blk', downward)  2.93 us
  transfers between devices with their start and end apart: 7, of which 4 were waited for; matrix products, arithmetic and copies ran while one was open for 0% of the time, Pallas kernels for 7%

profile of v1, /device:TPU:32, one launch (start us, length us, event | category | flops | bytes accessed | tf_op | source)
XLA Modules:
  0.0 80.6 jit_solution(10562805576620025604)
XLA Ops:
  0.0 12.5 %walker.1 = f32[256,256]{1,0:T(8,128)} custom-call(f32[1024,1024]{1,0:T(8,128)} %bitcast.12, bf16[4,1024,256]{2,1,0:T(8,128)(2,1)} %bitcast.13, s32[4,256]{1,0:T(4,128)} %bitcast.15, f32[1024,256]{1,0:T(8,128)} %l_hbm.1, f32[1024,256]{1,0:T(8,128)} %r_hbm.1), custom_call_target="tpu_custom_call" | custom-call | tf_op jit(solution)/shard_map/walker/pallas_call | solution.py:88
  12.6 21.8 %all_to_all.10.x_ref = f32[32,8,256]{2,1,0:T(8,128)S(1)} all-to-all(f32[32,8,256]{2,1,0:T(8,128)} %bitcast.14), channel_id=1, replica_groups=mesh['grp'=32,'blk'=8] {'grp'}, dimensions={0} | all-to-all | bytes 524288 | tf_op jit(solution)/shard_map/all_to_all | solution.py:220
  34.4 0.6 route.1
  34.9 16.2 %all_to_all.11 = f32[32,8,256]{2,1,0:T(8,128)S(1)} all-to-all(f32[32,8,256]{2,1,0:T(8,128)S(1)} %route.1), channel_id=1, replica_groups=mesh['grp'=32,'blk'=8] {'grp'}, dimensions={0} | all-to-all | bytes 524288 | tf_op jit(solution)/shard_map/all_to_all | solution.py:222
  51.1 1.6 %collective-permute-start = (f32[256,256]{1,0:T(8,128)S(1)}, f32[256,256]{1,0:T(8,128)S(1)}, u32[]{:S(2)}, u32[]{:S(2)}) collective-permute-start(f32[256,256]{1,0:T(8,128)S(1)} %bitcast.8), channel_id=1, source_target_pairs={{0,1},{1,2},{2,3},{3,0},{4,5},{5,6},{6,7},{7,4},{8,9},{9,10},{10,1... | collective-permute-start | bytes 786440 | tf_op jit(solution)/shard_map/ppermute | solution.py:190
  52.7 1.7 %collective-permute-start.1 = (f32[256,256]{1,0:T(8,128)S(1)}, f32[256,256]{1,0:T(8,128)S(1)}, u32[]{:S(2)}, u32[]{:S(2)}) collective-permute-start(f32[256,256]{1,0:T(8,128)S(1)} %bitcast.9), channel_id=1, source_target_pairs={{0,3},{1,0},{2,1},{3,2},{4,7},{5,4},{6,5},{7,6},{8,11},{9,8},{10,9... | collective-permute-start | bytes 786440 | tf_op jit(solution)/shard_map/ppermute | solution.py:191
  54.3 2.7 %collective-permute-start.2 = (f32[256,256]{1,0:T(8,128)S(1)}, f32[256,256]{1,0:T(8,128)S(1)}, u32[]{:S(2)}, u32[]{:S(2)}) collective-permute-start(f32[256,256]{1,0:T(8,128)S(1)} %bitcast.10), channel_id=1, source_target_pairs={{0,4},{1,5},{2,6},{3,7},{4,0},{5,1},{6,2},{7,3},{8,12},{9,13},{10,... | collective-permute-start | bytes 786440 | tf_op jit(solution)/shard_map/ppermute | solution.py:192
  57.1 0.8 %labels.1.pi_ref = bf16[1024,256]{1,0:T(8,128)(2,1)S(1)} custom-call(s32[4]{0:T(128)S(1)} %copy-done.3, s32[16,16]{1,0:T(8,128)S(1)} %copy-done.1, s32[32]{0:T(128)S(1)} %copy-done.4, s32[32]{0:T(128)S(1)} %copy-done.5), custom_call_target="tpu_custom_call" | custom-call | flops 4000000 | bytes 1000000 | tf_op jit(solution)/shard_map/labels/pallas_call | solution.py:138
  57.9 0.7 products_own.1.refs_3_
  58.7 1.0 %collective-permute-done.refs_0_ = f32[256,256]{1,0:T(8,128)S(1)} collective-permute-done((f32[256,256]{1,0:T(8,128)S(1)}, f32[256,256]{1,0:T(8,128)S(1)}, u32[]{:S(2)}, u32[]{:S(2)}) %collective-permute-start) | collective-permute-done | bytes 262176 | tf_op jit(solution)/shard_map/ppermute | solution.py:190
  59.6 0.0 collective-permute-done.1.refs_1_
  59.7 2.9 %collective-permute-done.2.refs_2_ = f32[256,256]{1,0:T(8,128)S(1)} collective-permute-done((f32[256,256]{1,0:T(8,128)S(1)}, f32[256,256]{1,0:T(8,128)S(1)}, u32[]{:S(2)}, u32[]{:S(2)}) %collective-permute-start.2) | collective-permute-done | bytes 262176 | tf_op jit(solution)/shard_map/ppermute | solution.py:192
  62.6 0.1 pad_maximum_fusion
  62.7 0.4 collective-permute-start.3
  63.1 2.9 %collective-permute-start.5 = (f32[384,256]{1,0:T(8,128)S(1)}, f32[384,256]{1,0:T(8,128)S(1)}, u32[]{:S(2)}, u32[]{:S(2)}) collective-permute-start(f32[384,256]{1,0:T(8,128)S(1)} %get-tuple-element.13), channel_id=1, source_target_pairs={{0,3},{1,0},{2,1},{3,2},{4,7},{5,4},{6,5},{7,6},{8,11},{9,8},{10,9... | collective-permute-start | bytes 1179656 | tf_op jit(solution)/shard_map/ppermute | solution.py:196
  66.0 1.9 %products_near.1.refs_2_ = f32[4,256,256]{2,1,0:T(8,128)S(1)} custom-call(bf16[1024,256]{1,0:T(8,128)(2,1)S(1)} %labels.1.pi_ref, f32[256,256]{1,0:T(8,128)S(1)} %collective-permute-done.refs_0_, f32[256,256]{1,0:T(8,128)S(1)} %collective-permute-done.1.refs_1_, f32[256,256]{1,0:T(8,128)S(1)} %collective-permute-done.2.refs_2_, ...), custom_call_target="tpu_custom_call" | custom-call | flops 1610612736 | bytes 2883584 | tf_op jit(solution)/shard_map/products_near/pallas_call | solution.py:171
  68.0 4.7 %collective-permute-done.3.refs_0_ = f32[384,256]{1,0:T(8,128)S(1)} collective-permute-done((f32[384,256]{1,0:T(8,128)S(1)}, f32[384,256]{1,0:T(8,128)S(1)}, u32[]{:S(2)}, u32[]{:S(2)}) %collective-permute-start.3) | collective-permute-done | bytes 393248 | tf_op jit(solution)/shard_map/ppermute | solution.py:195
  72.7 0.1 collective-permute-start.4
  72.8 0.0 collective-permute-done.5.refs_1_
  72.8 3.3 %collective-permute-start.6 = (f32[128,256]{1,0:T(8,128)S(1)}, f32[128,256]{1,0:T(8,128)S(1)}, u32[]{:S(2)}, u32[]{:S(2)}) collective-permute-start(f32[128,256]{1,0:T(8,128)S(1)} %slice.17), channel_id=1, source_target_pairs={{0,3},{1,0},{2,1},{3,2},{4,7},{5,4},{6,5},{7,6},{8,11},{9,8},{10,9... | collective-permute-start | bytes 393224 | tf_op jit(solution)/shard_map/ppermute | solution.py:201
  76.1 1.9 %products_beside.1.refs_2_ = f32[4,256,256]{2,1,0:T(8,128)S(1)} custom-call(bf16[1024,256]{1,0:T(8,128)(2,1)S(1)} %labels.1.pi_ref, f32[384,256]{1,0:T(8,128)S(1)} %collective-permute-done.3.refs_0_, f32[384,256]{1,0:T(8,128)S(1)} %collective-permute-done.5.refs_1_, f32[4,256,256]{2,1,0:T(8,128)S(1)} %products_near.1.refs_2_), custom_call_target="tpu_custom_call" | custom-call | flops 1610612736 | bytes 2883584 | tf_op jit(solution)/shard_map/products_beside/pallas_call | solution.py:171
  78.0 0.9 %collective-permute-done.4.refs_0_ = f32[128,256]{1,0:T(8,128)S(1)} collective-permute-done((f32[128,256]{1,0:T(8,128)S(1)}, f32[128,256]{1,0:T(8,128)S(1)}, u32[]{:S(2)}, u32[]{:S(2)}) %collective-permute-start.4) | collective-permute-done | bytes 131104 | tf_op jit(solution)/shard_map/ppermute | solution.py:200
  78.9 0.0 collective-permute-done.6.refs_1_
  78.9 1.7 %products_far.1 = f32[4,256,256]{2,1,0:T(8,128)} custom-call(bf16[1024,256]{1,0:T(8,128)(2,1)S(1)} %labels.1.pi_ref, f32[128,256]{1,0:T(8,128)S(1)} %collective-permute-done.4.refs_0_, f32[128,256]{1,0:T(8,128)S(1)} %collective-permute-done.6.refs_1_, f32[4,256,256]{2,1,0:T(8,128)S(1)} %products_beside.1.refs_2_), custom_call_target="tpu_custom_call" | custom-call | flops 536870912 | bytes 2359296 | tf_op jit(solution)/shard_map/products_far/pallas_call | solution.py:171
  (16 shorter events, 0.1 us)
Async XLA Ops:
  0.0 34.4 %copy-start.2 = (s32[1,32]{1,0:T(1,128)S(1)}, s32[1,32]{1,0:T(1,128)}, u32[]{:S(2)}) copy-start(s32[1,32]{1,0:T(1,128)} %targets_ref.1) | copy-start | bytes 388
  0.0 57.1 %copy-start.1 = (s32[16,16]{1,0:T(8,128)S(1)}, s32[16,16]{1,0:T(8,128)}, u32[]{:S(2)}) copy-start(s32[16,16]{1,0:T(8,128)} %ms_ref.1) | copy-start | bytes 3076
  0.0 57.1 %copy-start.3 = (s32[4]{0:T(128)S(1)}, s32[4]{0:T(128)}, u32[]{:S(2)}) copy-start(s32[4]{0:T(128)} %own_ref.1) | copy-start | bytes 52
  0.0 57.1 %copy-start.4 = (s32[32]{0:T(128)S(1)}, s32[32]{0:T(128)}, u32[]{:S(2)}) copy-start(s32[32]{0:T(128)} %tm_ref.1) | copy-start | bytes 388
  0.0 57.1 %copy-start.5 = (s32[32]{0:T(128)S(1)}, s32[32]{0:T(128)}, u32[]{:S(2)}) copy-start(s32[32]{0:T(128)} %tf_ref.1) | copy-start | bytes 388
  0.0 57.9 %copy-start = (f32[1,4,256,256]{3,2,1,0:T(8,128)S(1)}, f32[1,4,256,256]{3,2,1,0:T(8,128)}, u32[]{:S(2)}) copy-start(f32[1,4,256,256]{3,2,1,0:T(8,128)} %param.21) | copy-start | bytes 3145732
  51.1 8.5 %collective-permute-start = (f32[256,256]{1,0:T(8,128)S(1)}, f32[256,256]{1,0:T(8,128)S(1)}, u32[]{:S(2)}, u32[]{:S(2)}) collective-permute-start(f32[256,256]{1,0:T(8,128)S(1)} %bitcast.8), channel_id=1, source_target_pairs={{0,1},{1,2},{2,3},{3,0},{4,5},{5,6},{6,7},{7,4},{8,9},{9,10},{10,1... | collective-permute-start | bytes 786440 | tf_op jit(solution)/shard_map/ppermute | solution.py:190
  52.7 7.0 %collective-permute-start.1 = (f32[256,256]{1,0:T(8,128)S(1)}, f32[256,256]{1,0:T(8,128)S(1)}, u32[]{:S(2)}, u32[]{:S(2)}) collective-permute-start(f32[256,256]{1,0:T(8,128)S(1)} %bitcast.9), channel_id=1, source_target_pairs={{0,3},{1,0},{2,1},{3,2},{4,7},{5,4},{6,5},{7,6},{8,11},{9,8},{10,9... | collective-permute-start | bytes 786440 | tf_op jit(solution)/shard_map/ppermute | solution.py:191
  54.3 8.3 %collective-permute-start.2 = (f32[256,256]{1,0:T(8,128)S(1)}, f32[256,256]{1,0:T(8,128)S(1)}, u32[]{:S(2)}, u32[]{:S(2)}) collective-permute-start(f32[256,256]{1,0:T(8,128)S(1)} %bitcast.10), channel_id=1, source_target_pairs={{0,4},{1,5},{2,6},{3,7},{4,0},{5,1},{6,2},{7,3},{8,12},{9,13},{10,... | collective-permute-start | bytes 786440 | tf_op jit(solution)/shard_map/ppermute | solution.py:192
  62.7 9.9 %collective-permute-start.3 = (f32[384,256]{1,0:T(8,128)S(1)}, f32[384,256]{1,0:T(8,128)S(1)}, u32[]{:S(2)}, u32[]{:S(2)}) collective-permute-start(f32[384,256]{1,0:T(8,128)S(1)} %get-tuple-element.14), channel_id=1, source_target_pairs={{0,1},{1,2},{2,3},{3,0},{4,5},{5,6},{6,7},{7,4},{8,9},{9,10},{10,1... | collective-permute-start | bytes 1179656 | tf_op jit(solution)/shard_map/ppermute | solution.py:195
  63.1 9.7 %collective-permute-start.5 = (f32[384,256]{1,0:T(8,128)S(1)}, f32[384,256]{1,0:T(8,128)S(1)}, u32[]{:S(2)}, u32[]{:S(2)}) collective-permute-start(f32[384,256]{1,0:T(8,128)S(1)} %get-tuple-element.13), channel_id=1, source_target_pairs={{0,3},{1,0},{2,1},{3,2},{4,7},{5,4},{6,5},{7,6},{8,11},{9,8},{10,9... | collective-permute-start | bytes 1179656 | tf_op jit(solution)/shard_map/ppermute | solution.py:196
  72.7 6.3 %collective-permute-start.4 = (f32[128,256]{1,0:T(8,128)S(1)}, f32[128,256]{1,0:T(8,128)S(1)}, u32[]{:S(2)}, u32[]{:S(2)}) collective-permute-start(f32[128,256]{1,0:T(8,128)S(1)} %slice.16), channel_id=1, source_target_pairs={{0,1},{1,2},{2,3},{3,0},{4,5},{5,6},{6,7},{7,4},{8,9},{9,10},{10,1... | collective-permute-start | bytes 393224 | tf_op jit(solution)/shard_map/ppermute | solution.py:200
  72.8 6.1 %collective-permute-start.6 = (f32[128,256]{1,0:T(8,128)S(1)}, f32[128,256]{1,0:T(8,128)S(1)}, u32[]{:S(2)}, u32[]{:S(2)}) collective-permute-start(f32[128,256]{1,0:T(8,128)S(1)} %slice.17), channel_id=1, source_target_pairs={{0,3},{1,0},{2,1},{3,2},{4,7},{5,4},{6,5},{7,6},{8,11},{9,8},{10,9... | collective-permute-start | bytes 393224 | tf_op jit(solution)/shard_map/ppermute | solution.py:201

commit v2 on v1

--- a/solution.py
+++ b/solution.py
@@ -13,7 +13,7 @@
 NW = 16
 NK = 16
 KW = 256
-M_CHUNKS = 8
+M_CHUNKS = 2
 F32 = jnp.float32
 BF16 = jnp.bfloat16
 
@@ -35,53 +35,55 @@
     return lax.dot_general(a, b, (((1,), (1,)), ((), ())), preferred_element_type=F32)
 
 
-def walker_kernel(m_hbm, u_hbm, rows_hbm, l_hbm, r_hbm, out_ref, m_v, u_v, rows_v, l_v, r_v, w_ref, t_ref, sems):
+def mm_split(hi, lo, b):
+    count = hi.shape[0]
+    both = mm(jnp.concatenate([hi, lo]), b)
+    return both[:count] + both[count:]
+
+
+def walker_kernel(m_hbm, u_hbm, rows_hbm, l_hbm, r_hbm, out_ref, m_v, u_v, rows_v, l_v, r_v, p_ref, s_ref, sems):
     size = ORDER // M_CHUNKS
-    copy_l = pltpu.make_async_copy(l_hbm, l_v, sems.at[0])
-    copy_r = pltpu.make_async_copy(r_hbm, r_v, sems.at[1])
-    copy_u = [pltpu.make_async_copy(u_hbm.at[u], u_v.at[u], sems.at[2 + u]) for u in range(UPD)]
+    copy_rows = pltpu.make_async_copy(rows_hbm, rows_v, sems.at[0])
+    copy_l = pltpu.make_async_copy(l_hbm, l_v, sems.at[1])
+    copy_r = pltpu.make_async_copy(r_hbm, r_v, sems.at[2])
+    copy_u = [pltpu.make_async_copy(u_hbm.at[u], u_v.at[u], sems.at[3 + u]) for u in range(UPD)]
     copy_m = [
         pltpu.make_async_copy(
-            m_hbm.at[pl.ds(k * size, size), :], m_v.at[pl.ds(k * size, size), :], sems.at[2 + UPD + k]
+            m_hbm.at[pl.ds(k * size, size), :], m_v.at[pl.ds(k * size, size), :], sems.at[3 + UPD + k]
         )
         for k in range(M_CHUNKS)
     ]
-    copy_rows = pltpu.make_async_copy(rows_hbm, rows_v, sems.at[2 + UPD + M_CHUNKS])
-    copy_l.start()
-    copy_rows.start()
-    for u in reversed(range(UPD)):
-        copy_u[u].start()
-    for copy in copy_m:
+    for copy in (copy_rows, copy_r, *copy_m, copy_l, copy_u[3], copy_u[0], copy_u[2], copy_u[1]):
         copy.start()
-    copy_r.start()
 
     lane = lax.broadcasted_iota(jnp.int32, (RANK, ORDER), 1)
-    copy_l.wait()
     copy_rows.wait()
-    w_ref[...] = l_v[...].T
-    for u in reversed(range(UPD)):
+    for u in range(UPD):
         column = jnp.broadcast_to(rows_v[pl.ds(u, 1), :], (128, RANK)).T[:, :1]
-        chosen = jnp.where(lane == column, 1.0, 0.0).astype(BF16)
-        w_hi, w_lo = split(w_ref[...])
-        copy_u[u].wait()
-        x = mm(w_hi, u_v[u]) + mm(w_lo, u_v[u])
-        x_hi, x_lo = split(x)
-        w_ref[...] += mm(x_hi, chosen) + mm(x_lo, chosen)
-    w_hi, w_lo = split(w_ref[...])
+        s_ref[u] = jnp.where(lane == column, 1.0, 0.0).astype(BF16)
+
+    copy_r.wait()
+    r_hi, r_lo = split(r_v[...])
     for k in range(M_CHUNKS):
         copy_m[k].wait()
         m_hi, m_lo = split(m_v[pl.ds(k * size, size), :])
-        part_hi = w_hi[:, k * size : (k + 1) * size]
-        part_lo = w_lo[:, k * size : (k + 1) * size]
-        term = mm(part_hi, m_hi) + mm(part_lo, m_hi) + mm(part_hi, m_lo)
-        if k == 0:
-            t_ref[...] = term
-        else:
-            t_ref[...] += term
-    copy_r.wait()
-    t_hi, t_lo = split(t_ref[...])
-    r_hi, r_lo = split(r_v[...])
-    out_ref[...] = mm(t_hi, r_hi) + mm(t_lo, r_hi) + mm(t_hi, r_lo)
+        p_ref[pl.ds(k * size, size), :] = mm_split(m_hi, m_lo, r_hi) + mm(m_hi, r_lo)
+    copy_l.wait()
+    for copy in copy_u:
+        copy.wait()
+    right = p_ref[...]
+    left = l_v[...].T
+    for early, late in ((0, 3), (1, 2)):
+        right_hi, right_lo = split(right)
+        picked_hi = mm(s_ref[early], right_hi).astype(BF16)
+        picked_lo = mm(s_ref[early], right_lo).astype(BF16)
+        right = right + (mm(u_v[early], picked_hi) + mm(u_v[early], picked_lo))
+        left_hi, left_lo = split(left)
+        x_hi, x_lo = split(mm_split(left_hi, left_lo, u_v[late]))
+        left = left + mm_split(x_hi, x_lo, s_ref[late])
+    left_hi, left_lo = split(left)
+    right_hi, right_lo = split(right)
+    out_ref[...] = mm_split(left_hi, left_lo, right_hi) + mm(left_hi, right_lo)
 
 
 def walker(matrix, updates, rows, left, right):
@@ -96,8 +98,8 @@
             pltpu.VMEM((UPD, RANK), jnp.int32),
             pltpu.VMEM((ORDER, KW), F32),
             pltpu.VMEM((ORDER, KW), F32),
-            pltpu.VMEM((KW, ORDER), F32),
-            pltpu.VMEM((KW, ORDER), F32),
+            pltpu.VMEM((ORDER, KW), F32),
+            pltpu.VMEM((UPD, RANK, ORDER), BF16),
             pltpu.SemaphoreType.DMA((3 + UPD + M_CHUNKS,)),
         ],
         compiler_params=pltpu.CompilerParams(vmem_limit_bytes=60 << 20),
@@ -146,14 +148,16 @@
     )(ownership, momentum_sum, moments, freqs)
 
 
-def products_kernel(scale, picks, pi_ref, *refs):
-    *piece_refs, total_ref, out_ref = refs
+def products_kernel(scale, last, pi_ref, *refs):
+    if last:
+        *piece_refs, total_ref, out_hbm, out_v, sems = refs
+    else:
+        *piece_refs, total_ref, out_ref = refs
     held = total_ref.shape[0]
     pi = pi_ref[...]
     terms = [total_ref[j] for j in range(held)]
-    for pick in picks:
-        parts = [piece_refs[number][pl.ds(start, count), :] for number, start, count in pick]
-        a = parts[0] if len(parts) == 1 else jnp.concatenate(parts, axis=0)
+    for number, piece_ref in enumerate(piece_refs):
+        a = piece_ref[...]
         a_hi, a_lo = split(a)
         v_hi = mm_nt(pi, a_hi).astype(BF16)
         v_lo = mm_nt(pi, a_lo).astype(BF16)
@@ -161,18 +165,25 @@
         for j in range(held):
             rows = slice(j * KW, (j + 1) * KW)
             terms[j] += a * (mm_nt(v_hi[rows], pi[rows]) + mm_nt(v_lo[rows], pi[rows]))
+            if last and number == len(piece_refs) - 1:
+                out_v[j] = terms[j]
+                pltpu.make_async_copy(out_v.at[j], out_hbm.at[j], sems.at[j]).start()
     for j in range(held):
-        out_ref[j] = terms[j]
-
-
-def products(scale, pi, picks, pieces, total, name):
+        if last:
+            pltpu.make_async_copy(out_v.at[j], out_hbm.at[j], sems.at[j]).wait()
+        else:
+            out_ref[j] = terms[j]
+
+
+def products(scale, pi, pieces, total, name, last=False):
     held = total.shape[0]
-    count = len(picks)
-    return pl.pallas_call(
-        functools.partial(products_kernel, scale, picks),
+    count = len(pieces)
+    return pl.pallas_call(
+        functools.partial(products_kernel, scale, last),
         out_shape=jax.ShapeDtypeStruct(total.shape, F32),
-        in_specs=[VMEM] * (2 + len(pieces)),
-        out_specs=VMEM,
+        in_specs=[VMEM] * (2 + count),
+        out_specs=HBM if last else VMEM,
+        scratch_shapes=[pltpu.VMEM(total.shape, F32), pltpu.SemaphoreType.DMA((held,))] if last else [],
         cost_estimate=pl.CostEstimate(
             flops=count * held * 8 * KW**3, bytes_accessed=4 * KW * KW * (2 * held + count), transcendentals=0
         ),
@@ -182,32 +193,22 @@
 
 
 def cycle_products(scale, pi, own, prior):
-    half = KW // 2
-    whole = (0, KW)
     across = [(j, (j + 4) % 8) for j in range(8)]
     upward = [(j, j // 4 * 4 + (j % 4 + 1) % 4) for j in range(8)]
     downward = [(j, j // 4 * 4 + (j % 4 + 3) % 4) for j in range(8)]
+    opposite = [(j, j // 4 * 4 + (j % 4 + 2) % 4) for j in range(8)]
     below = lax.ppermute(own, "blk", upward)
     above = lax.ppermute(own, "blk", downward)
     beside = lax.ppermute(own, "blk", across)
-    total = products(scale, pi, [[(0, *whole)]], [own], prior, "products_own")
-    below, above, beside, total = lax.optimization_barrier((below, above, beside, total))
-    up = lax.ppermute(jnp.concatenate([beside, below[:half]]), "blk", upward)
-    down = lax.ppermute(jnp.concatenate([beside, above[half:]]), "blk", downward)
-    total = products(
-        scale, pi, [[(number, *whole)] for number in range(3)], [below, above, beside], total, "products_near"
-    )
-    far_up = lax.ppermute(up[:half], "blk", upward)
-    far_down = lax.ppermute(down[half:KW], "blk", downward)
-    total = products(
-        scale,
-        pi,
-        [[(0, *whole)], [(1, *whole)], [(0, KW, half), (1, KW, half)]],
-        [up, down],
-        total,
-        "products_beside",
-    )
-    return products(scale, pi, [[(0, 0, half), (1, 0, half)]], [far_up, far_down], total, "products_far")
+    far = lax.ppermute(own, "blk", opposite)
+    total = products(scale, pi, [own], prior, "products_own")
+    below, above, beside, far, total = lax.optimization_barrier((below, above, beside, far, total))
+    beside_below = lax.ppermute(beside, "blk", upward)
+    beside_above = lax.ppermute(beside, "blk", downward)
+    beside_far = lax.ppermute(far, "blk", across)
+    total = products(scale, pi, [below, above, beside, far], total, "products_near")
+    total = products(scale, pi, [beside_below, beside_above], total, "products_beside")
+    return products(scale, pi, [beside_far], total, "products_far", last=True)
 
 
 def shards(

time: 82.3 us -> 78.7 us (0.956)
  the two profiles are of different devices: /device:TPU:32 before, /device:TPU:4 now
where the time goes in v2:
time: 78.7 us; the launch traced here: 78.5 us
  blocking collectives  38.8 us (49%)
  Pallas kernels  16.9 us (21%)
  waiting for transfers between devices  12.9 us (16%)
  starting transfers between devices  9.45 us (12%)
    all_to_all x1, blocking collectives, shards(): lax.all_to_all(greens.reshape(n_grp, KW // n_grp, KW), 'grp', 0, 0, tiled...  22.7 us
    all_to_all x1, blocking collectives, shards(): measured = lax.all_to_all(routed, 'grp', 0, 0, tiled=True).reshape(KW, KW)  16.2 us
    pallas_call x1, Pallas kernels, walker(): pl.pallas_call(walker_kernel, out_shape=jax.ShapeDtypeStruct((KW, KW), F3...  9.32 us
    pallas_call x4, Pallas kernels, products(): pl.pallas_call(functools.partial(products_kernel, scale, last), out_shape...  6.23 us
    ppermute x1, waiting for transfers between devices, cycle_products(): beside_below = lax.ppermute(beside, 'blk', upward)  3.41 us
    ppermute x1, starting transfers between devices, cycle_products(): far = lax.ppermute(own, 'blk', opposite)  3.19 us
    ppermute x1, waiting for transfers between devices, cycle_products(): far = lax.ppermute(own, 'blk', opposite)  3.12 us
    ppermute x1, waiting for transfers between devices, cycle_products(): above = lax.ppermute(own, 'blk', downward)  3.09 us
  transfers between devices with their start and end apart: 7, of which 5 were waited for; matrix products, arithmetic and copies ran while one was open for 0% of the time, Pallas kernels for 7%

profile of v2, /device:TPU:4, one launch (start us, length us, event | category | flops | bytes accessed | tf_op | source)
XLA Modules:
  0.0 78.5 jit_solution(1613434665085031400)
XLA Ops:
  0.0 9.3 %walker.1 = f32[256,256]{1,0:T(8,128)} custom-call(f32[1024,1024]{1,0:T(8,128)} %bitcast.13, bf16[4,1024,256]{2,1,0:T(8,128)(2,1)} %bitcast.14, s32[4,256]{1,0:T(4,128)} %bitcast.16, f32[1024,256]{1,0:T(8,128)} %l_hbm.1, f32[1024,256]{1,0:T(8,128)} %r_hbm.1), custom_call_target="tpu_custom_call" | custom-call | tf_op jit(solution)/shard_map/walker/pallas_call | solution.py:90
  9.4 22.7 %all_to_all.10.x_ref = f32[32,8,256]{2,1,0:T(8,128)S(1)} all-to-all(f32[32,8,256]{2,1,0:T(8,128)} %bitcast.15), channel_id=1, replica_groups=mesh['grp'=32,'blk'=8] {'grp'}, dimensions={0} | all-to-all | bytes 524288 | tf_op jit(solution)/shard_map/all_to_all | solution.py:221
  32.0 0.6 route.1
  32.6 16.2 %all_to_all.11 = f32[32,8,256]{2,1,0:T(8,128)S(1)} all-to-all(f32[32,8,256]{2,1,0:T(8,128)S(1)} %route.1), channel_id=1, replica_groups=mesh['grp'=32,'blk'=8] {'grp'}, dimensions={0} | all-to-all | bytes 524288 | tf_op jit(solution)/shard_map/all_to_all | solution.py:223
  48.8 3.2 %collective-permute-start.3 = (f32[256,256]{1,0:T(8,128)S(1)}, f32[256,256]{1,0:T(8,128)S(1)}, u32[]{:S(2)}, u32[]{:S(2)}) collective-permute-start(f32[256,256]{1,0:T(8,128)S(1)} %bitcast.8), channel_id=1, source_target_pairs={{0,2},{1,3},{2,0},{3,1},{4,6},{5,7},{6,4},{7,5},{8,10},{9,11},{10,... | collective-permute-start | bytes 786440 | tf_op jit(solution)/shard_map/ppermute | solution.py:203
  52.0 0.8 %collective-permute-start.2 = (f32[256,256]{1,0:T(8,128)S(1)}, f32[256,256]{1,0:T(8,128)S(1)}, u32[]{:S(2)}, u32[]{:S(2)}) collective-permute-start(f32[256,256]{1,0:T(8,128)S(1)} %bitcast.9), channel_id=1, source_target_pairs={{0,4},{1,5},{2,6},{3,7},{4,0},{5,1},{6,2},{7,3},{8,12},{9,13},{10,... | collective-permute-start | bytes 786440 | tf_op jit(solution)/shard_map/ppermute | solution.py:202
  52.8 1.1 %collective-permute-start.1 = (f32[256,256]{1,0:T(8,128)S(1)}, f32[256,256]{1,0:T(8,128)S(1)}, u32[]{:S(2)}, u32[]{:S(2)}) collective-permute-start(f32[256,256]{1,0:T(8,128)S(1)} %bitcast.10), channel_id=1, source_target_pairs={{0,3},{1,0},{2,1},{3,2},{4,7},{5,4},{6,5},{7,6},{8,11},{9,8},{10,9... | collective-permute-start | bytes 786440 | tf_op jit(solution)/shard_map/ppermute | solution.py:201
  53.8 1.0 %collective-permute-start = (f32[256,256]{1,0:T(8,128)S(1)}, f32[256,256]{1,0:T(8,128)S(1)}, u32[]{:S(2)}, u32[]{:S(2)}) collective-permute-start(f32[256,256]{1,0:T(8,128)S(1)} %bitcast.11), channel_id=1, source_target_pairs={{0,1},{1,2},{2,3},{3,0},{4,5},{5,6},{6,7},{7,4},{8,9},{9,10},{10,1... | collective-permute-start | bytes 786440 | tf_op jit(solution)/shard_map/ppermute | solution.py:200
  54.8 0.0 copy-done.3
  54.8 0.8 %labels.1.pi_ref = bf16[1024,256]{1,0:T(8,128)(2,1)S(1)} custom-call(s32[4]{0:T(128)S(1)} %copy-done.3, s32[16,16]{1,0:T(8,128)S(1)} %copy-done.1, s32[32]{0:T(128)S(1)} %copy-done.4, s32[32]{0:T(128)S(1)} %copy-done.5), custom_call_target="tpu_custom_call" | custom-call | flops 4000000 | bytes 1000000 | tf_op jit(solution)/shard_map/labels/pallas_call | solution.py:140
  55.7 0.8 products_own.1.refs_4_
  56.4 3.1 %collective-permute-done.3.refs_3_ = f32[256,256]{1,0:T(8,128)S(1)} collective-permute-done((f32[256,256]{1,0:T(8,128)S(1)}, f32[256,256]{1,0:T(8,128)S(1)}, u32[]{:S(2)}, u32[]{:S(2)}) %collective-permute-start.3) | collective-permute-done | bytes 262176 | tf_op jit(solution)/shard_map/ppermute | solution.py:203
  59.5 0.9 %collective-permute-done.2.refs_2_ = f32[256,256]{1,0:T(8,128)S(1)} collective-permute-done((f32[256,256]{1,0:T(8,128)S(1)}, f32[256,256]{1,0:T(8,128)S(1)}, u32[]{:S(2)}, u32[]{:S(2)}) %collective-permute-start.2) | collective-permute-done | bytes 262176 | tf_op jit(solution)/shard_map/ppermute | solution.py:202
  60.4 3.1 %collective-permute-done.1.refs_1_ = f32[256,256]{1,0:T(8,128)S(1)} collective-permute-done((f32[256,256]{1,0:T(8,128)S(1)}, f32[256,256]{1,0:T(8,128)S(1)}, u32[]{:S(2)}, u32[]{:S(2)}) %collective-permute-start.1) | collective-permute-done | bytes 262176 | tf_op jit(solution)/shard_map/ppermute | solution.py:201
  63.5 0.0 collective-permute-done.refs_0_
  63.5 2.6 %collective-permute-start.6 = (f32[256,256]{1,0:T(8,128)S(1)}, f32[256,256]{1,0:T(8,128)S(1)}, u32[]{:S(2)}, u32[]{:S(2)}) collective-permute-start(f32[256,256]{1,0:T(8,128)S(1)} %collective-permute-done.2.refs_2_), channel_id=1, source_target_pairs={{0,3},{1,0},{2,1},{3,2},{4,7},{5,4},{6,5},{7,6},{8,11},{9,8},{10,9... | collective-permute-start | bytes 786440 | tf_op jit(solution)/shard_map/ppermute | solution.py:207
  66.2 0.0 collective-permute-start.5
  66.2 0.8 %collective-permute-start.4 = (f32[256,256]{1,0:T(8,128)S(1)}, f32[256,256]{1,0:T(8,128)S(1)}, u32[]{:S(2)}, u32[]{:S(2)}) collective-permute-start(f32[256,256]{1,0:T(8,128)S(1)} %collective-permute-done.3.refs_3_), channel_id=1, source_target_pairs={{0,4},{1,5},{2,6},{3,7},{4,0},{5,1},{6,2},{7,3},{8,12},{9,13},{10,... | collective-permute-start | bytes 786440 | tf_op jit(solution)/shard_map/ppermute | solution.py:208
  67.0 2.5 %products_near.1.refs_2_ = f32[4,256,256]{2,1,0:T(8,128)S(1)} custom-call(bf16[1024,256]{1,0:T(8,128)(2,1)S(1)} %labels.1.pi_ref, f32[256,256]{1,0:T(8,128)S(1)} %collective-permute-done.refs_0_, f32[256,256]{1,0:T(8,128)S(1)} %collective-permute-done.1.refs_1_, f32[256,256]{1,0:T(8,128)S(1)} %collective-permute-done.2.refs_2_, ...), custom_call_target="tpu_custom_call" | custom-call | flops 2147483648 | bytes 3145728 | tf_op jit(solution)/shard_map/products_near/pallas_call | solution.py:181
  69.5 2.4 %collective-permute-done.6.refs_1_ = f32[256,256]{1,0:T(8,128)S(1)} collective-permute-done((f32[256,256]{1,0:T(8,128)S(1)}, f32[256,256]{1,0:T(8,128)S(1)}, u32[]{:S(2)}, u32[]{:S(2)}) %collective-permute-start.6) | collective-permute-done | bytes 262176 | tf_op jit(solution)/shard_map/ppermute | solution.py:207
  71.9 3.4 %collective-permute-done.5.refs_0_ = f32[256,256]{1,0:T(8,128)S(1)} collective-permute-done((f32[256,256]{1,0:T(8,128)S(1)}, f32[256,256]{1,0:T(8,128)S(1)}, u32[]{:S(2)}, u32[]{:S(2)}) %collective-permute-start.5) | collective-permute-done | bytes 262176 | tf_op jit(solution)/shard_map/ppermute | solution.py:206
  75.3 1.3 %products_beside.1.refs_1_ = f32[4,256,256]{2,1,0:T(8,128)S(1)} custom-call(bf16[1024,256]{1,0:T(8,128)(2,1)S(1)} %labels.1.pi_ref, f32[256,256]{1,0:T(8,128)S(1)} %collective-permute-done.5.refs_0_, f32[256,256]{1,0:T(8,128)S(1)} %collective-permute-done.6.refs_1_, f32[4,256,256]{2,1,0:T(8,128)S(1)} %products_near.1.refs_2_), custom_call_target="tpu_custom_call" | custom-call | flops 1073741824 | bytes 2621440 | tf_op jit(solution)/shard_map/products_beside/pallas_call | solution.py:181
  76.7 0.0 collective-permute-done.4.refs_0_
  76.7 1.6 %products_far.1 = f32[4,256,256]{2,1,0:T(8,128)} custom-call(bf16[1024,256]{1,0:T(8,128)(2,1)S(1)} %labels.1.pi_ref, f32[256,256]{1,0:T(8,128)S(1)} %collective-permute-done.4.refs_0_, f32[4,256,256]{2,1,0:T(8,128)S(1)} %products_beside.1.refs_1_), custom_call_target="tpu_custom_call" | custom-call | flops 536870912 | bytes 2359296 | tf_op jit(solution)/shard_map/products_far/pallas_call | solution.py:181
  (11 shorter events, 0.0 us)
Async XLA Ops:
  0.0 32.0 %copy-start.2 = (s32[1,32]{1,0:T(1,128)S(1)}, s32[1,32]{1,0:T(1,128)}, u32[]{:S(2)}) copy-start(s32[1,32]{1,0:T(1,128)} %targets_ref.1) | copy-start | bytes 388
  0.0 54.8 %copy-start.1 = (s32[16,16]{1,0:T(8,128)S(1)}, s32[16,16]{1,0:T(8,128)}, u32[]{:S(2)}) copy-start(s32[16,16]{1,0:T(8,128)} %ms_ref.1) | copy-start | bytes 3076
  0.0 54.8 %copy-start.3 = (s32[4]{0:T(128)S(1)}, s32[4]{0:T(128)}, u32[]{:S(2)}) copy-start(s32[4]{0:T(128)} %own_ref.1) | copy-start | bytes 52
  0.0 54.8 %copy-start.4 = (s32[32]{0:T(128)S(1)}, s32[32]{0:T(128)}, u32[]{:S(2)}) copy-start(s32[32]{0:T(128)} %tm_ref.1) | copy-start | bytes 388
  0.0 54.8 %copy-start.5 = (s32[32]{0:T(128)S(1)}, s32[32]{0:T(128)}, u32[]{:S(2)}) copy-start(s32[32]{0:T(128)} %tf_ref.1) | copy-start | bytes 388
  0.0 55.6 %copy-start = (f32[1,4,256,256]{3,2,1,0:T(8,128)S(1)}, f32[1,4,256,256]{3,2,1,0:T(8,128)}, u32[]{:S(2)}) copy-start(f32[1,4,256,256]{3,2,1,0:T(8,128)} %param.21) | copy-start | bytes 3145732
  48.8 10.8 %collective-permute-start.3 = (f32[256,256]{1,0:T(8,128)S(1)}, f32[256,256]{1,0:T(8,128)S(1)}, u32[]{:S(2)}, u32[]{:S(2)}) collective-permute-start(f32[256,256]{1,0:T(8,128)S(1)} %bitcast.8), channel_id=1, source_target_pairs={{0,2},{1,3},{2,0},{3,1},{4,6},{5,7},{6,4},{7,5},{8,10},{9,11},{10,... | collective-permute-start | bytes 786440 | tf_op jit(solution)/shard_map/ppermute | solution.py:203
  52.0 8.5 %collective-permute-start.2 = (f32[256,256]{1,0:T(8,128)S(1)}, f32[256,256]{1,0:T(8,128)S(1)}, u32[]{:S(2)}, u32[]{:S(2)}) collective-permute-start(f32[256,256]{1,0:T(8,128)S(1)} %bitcast.9), channel_id=1, source_target_pairs={{0,4},{1,5},{2,6},{3,7},{4,0},{5,1},{6,2},{7,3},{8,12},{9,13},{10,... | collective-permute-start | bytes 786440 | tf_op jit(solution)/shard_map/ppermute | solution.py:202
  52.8 10.7 %collective-permute-start.1 = (f32[256,256]{1,0:T(8,128)S(1)}, f32[256,256]{1,0:T(8,128)S(1)}, u32[]{:S(2)}, u32[]{:S(2)}) collective-permute-start(f32[256,256]{1,0:T(8,128)S(1)} %bitcast.10), channel_id=1, source_target_pairs={{0,3},{1,0},{2,1},{3,2},{4,7},{5,4},{6,5},{7,6},{8,11},{9,8},{10,9... | collective-permute-start | bytes 786440 | tf_op jit(solution)/shard_map/ppermute | solution.py:201
  53.8 9.7 %collective-permute-start = (f32[256,256]{1,0:T(8,128)S(1)}, f32[256,256]{1,0:T(8,128)S(1)}, u32[]{:S(2)}, u32[]{:S(2)}) collective-permute-start(f32[256,256]{1,0:T(8,128)S(1)} %bitcast.11), channel_id=1, source_target_pairs={{0,1},{1,2},{2,3},{3,0},{4,5},{5,6},{6,7},{7,4},{8,9},{9,10},{10,1... | collective-permute-start | bytes 786440 | tf_op jit(solution)/shard_map/ppermute | solution.py:200
  63.5 8.4 %collective-permute-start.6 = (f32[256,256]{1,0:T(8,128)S(1)}, f32[256,256]{1,0:T(8,128)S(1)}, u32[]{:S(2)}, u32[]{:S(2)}) collective-permute-start(f32[256,256]{1,0:T(8,128)S(1)} %collective-permute-done.2.refs_2_), channel_id=1, source_target_pairs={{0,3},{1,0},{2,1},{3,2},{4,7},{5,4},{6,5},{7,6},{8,11},{9,8},{10,9... | collective-permute-start | bytes 786440 | tf_op jit(solution)/shard_map/ppermute | solution.py:207
  66.2 9.2 %collective-permute-start.5 = (f32[256,256]{1,0:T(8,128)S(1)}, f32[256,256]{1,0:T(8,128)S(1)}, u32[]{:S(2)}, u32[]{:S(2)}) collective-permute-start(f32[256,256]{1,0:T(8,128)S(1)} %collective-permute-done.2.refs_2_), channel_id=1, source_target_pairs={{0,1},{1,2},{2,3},{3,0},{4,5},{5,6},{6,7},{7,4},{8,9},{9,10},{10,1... | collective-permute-start | bytes 786440 | tf_op jit(solution)/shard_map/ppermute | solution.py:206
  66.2 10.5 %collective-permute-start.4 = (f32[256,256]{1,0:T(8,128)S(1)}, f32[256,256]{1,0:T(8,128)S(1)}, u32[]{:S(2)}, u32[]{:S(2)}) collective-permute-start(f32[256,256]{1,0:T(8,128)S(1)} %collective-permute-done.3.refs_3_), channel_id=1, source_target_pairs={{0,4},{1,5},{2,6},{3,7},{4,0},{5,1},{6,2},{7,3},{8,12},{9,13},{10,... | collective-permute-start | bytes 786440 | tf_op jit(solution)/shard_map/ppermute | solution.py:208

commit v3 on v2

--- a/solution.py
+++ b/solution.py
@@ -102,9 +102,9 @@
             pltpu.VMEM((UPD, RANK, ORDER), BF16),
             pltpu.SemaphoreType.DMA((3 + UPD + M_CHUNKS,)),
         ],
-        compiler_params=pltpu.CompilerParams(vmem_limit_bytes=60 << 20),
+        compiler_params=pltpu.CompilerParams(vmem_limit_bytes=24 << 20),
         name="walker",
-    )(matrix, updates, rows, left, right)
+    )(*(pltpu.with_memory_space_constraint(x, pltpu.HBM) for x in (matrix, updates, rows, left, right)))
 
 
 def route_kernel(n, targets_ref, x_ref, out_ref):
@@ -202,11 +202,12 @@
     beside = lax.ppermute(own, "blk", across)
     far = lax.ppermute(own, "blk", opposite)
     total = products(scale, pi, [own], prior, "products_own")
-    below, above, beside, far, total = lax.optimization_barrier((below, above, beside, far, total))
+    beside, total = lax.optimization_barrier((beside, total))
     beside_below = lax.ppermute(beside, "blk", upward)
     beside_above = lax.ppermute(beside, "blk", downward)
+    far, total = lax.optimization_barrier((far, total))
     beside_far = lax.ppermute(far, "blk", across)
-    total = products(scale, pi, [below, above, beside, far], total, "products_near")
+    total = products(scale, pi, [beside, far, below, above], total, "products_near")
     total = products(scale, pi, [beside_below, beside_above], total, "products_beside")
     return products(scale, pi, [beside_far], total, "products_far", last=True)
 

time: 78.7 us -> 74.2 us (0.943)
  the two profiles are of different devices: /device:TPU:4 before, /device:TPU:32 now
where the time goes in v3:
time: 74.2 us; the launch traced here: 73 us
  blocking collectives  37.8 us (51%)
  Pallas kernels  16.3 us (22%)
  starting transfers between devices  11.3 us (15%)
  waiting for transfers between devices  7.36 us (10%)
    all_to_all x1, blocking collectives, shards(): lax.all_to_all(greens.reshape(n_grp, KW // n_grp, KW), 'grp', 0, 0, tiled...  21.6 us
    all_to_all x1, blocking collectives, shards(): measured = lax.all_to_all(routed, 'grp', 0, 0, tiled=True).reshape(KW, KW)  16.2 us
    pallas_call x1, Pallas kernels, walker(): pl.pallas_call(walker_kernel, out_shape=jax.ShapeDtypeStruct((KW, KW), F3...  8.62 us
    pallas_call x4, Pallas kernels, products(): pl.pallas_call(functools.partial(products_kernel, scale, last), out_shape...  6.24 us
    ppermute x1, waiting for transfers between devices, cycle_products(): above = lax.ppermute(own, 'blk', downward)  4.95 us
    ppermute x1, starting transfers between devices, cycle_products(): far = lax.ppermute(own, 'blk', opposite)  3.19 us
    ppermute x1, starting transfers between devices, cycle_products(): beside = lax.ppermute(own, 'blk', across)  2.73 us
    ppermute x1, starting transfers between devices, cycle_products(): beside_above = lax.ppermute(beside, 'blk', downward)  2.34 us
  transfers between devices with their start and end apart: 7, of which 3 were waited for; matrix products, arithmetic and copies ran while one was open for 0% of the time, Pallas kernels for 7%

profile of v3, /device:TPU:32, one launch (start us, length us, event | category | flops | bytes accessed | tf_op | source)
XLA Modules:
  0.0 73.0 jit_solution(4253705063242089058)
XLA Ops:
  0.0 0.0 copy-start.4
  0.0 8.6 %walker.1 = f32[256,256]{1,0:T(8,128)S(1)} custom-call(f32[1024,1024]{1,0:T(8,128)} %bitcast.14, bf16[4,1024,256]{2,1,0:T(8,128)(2,1)} %bitcast.15, s32[4,256]{1,0:T(4,128)} %bitcast.16, f32[1024,256]{1,0:T(8,128)} %l_hbm.1, f32[1024,256]{1,0:T(8,128)} %r_hbm.1), custom_call_target="tpu_custom_call" | custom-call | tf_op jit(solution)/shard_map/walker/pallas_call | solution.py:90
  8.7 21.6 %all_to_all.10.x_ref = f32[32,8,256]{2,1,0:T(8,128)S(1)} all-to-all(f32[32,8,256]{2,1,0:T(8,128)S(1)} %bitcast.7), channel_id=1, replica_groups=mesh['grp'=32,'blk'=8] {'grp'}, dimensions={0} | all-to-all | bytes 524288 | tf_op jit(solution)/shard_map/all_to_all | solution.py:222
  30.3 0.6 route.1
  30.8 16.2 %all_to_all.11 = f32[32,8,256]{2,1,0:T(8,128)S(1)} all-to-all(f32[32,8,256]{2,1,0:T(8,128)S(1)} %route.1), channel_id=1, replica_groups=mesh['grp'=32,'blk'=8] {'grp'}, dimensions={0} | all-to-all | bytes 524288 | tf_op jit(solution)/shard_map/all_to_all | solution.py:224
  47.0 2.7 %collective-permute-start.1 = (f32[256,256]{1,0:T(8,128)S(1)}, f32[256,256]{1,0:T(8,128)S(1)}, u32[]{:S(2)}, u32[]{:S(2)}) collective-permute-start(f32[256,256]{1,0:T(8,128)S(1)} %bitcast.9), channel_id=1, source_target_pairs={{0,4},{1,5},{2,6},{3,7},{4,0},{5,1},{6,2},{7,3},{8,12},{9,13},{10,... | collective-permute-start | bytes 786440 | tf_op jit(solution)/shard_map/ppermute | solution.py:202
  49.7 3.2 %collective-permute-start = (f32[256,256]{1,0:T(8,128)S(1)}, f32[256,256]{1,0:T(8,128)S(1)}, u32[]{:S(2)}, u32[]{:S(2)}) collective-permute-start(f32[256,256]{1,0:T(8,128)S(1)} %bitcast.10), channel_id=1, source_target_pairs={{0,2},{1,3},{2,0},{3,1},{4,6},{5,7},{6,4},{7,5},{8,10},{9,11},{10,... | collective-permute-start | bytes 786440 | tf_op jit(solution)/shard_map/ppermute | solution.py:203
  52.9 1.1 %collective-permute-start.6 = (f32[256,256]{1,0:T(8,128)S(1)}, f32[256,256]{1,0:T(8,128)S(1)}, u32[]{:S(2)}, u32[]{:S(2)}) collective-permute-start(f32[256,256]{1,0:T(8,128)S(1)} %bitcast.11), channel_id=1, source_target_pairs={{0,3},{1,0},{2,1},{3,2},{4,7},{5,4},{6,5},{7,6},{8,11},{9,8},{10,9... | collective-permute-start | bytes 786440 | tf_op jit(solution)/shard_map/ppermute | solution.py:201
  54.0 1.0 %collective-permute-start.5 = (f32[256,256]{1,0:T(8,128)S(1)}, f32[256,256]{1,0:T(8,128)S(1)}, u32[]{:S(2)}, u32[]{:S(2)}) collective-permute-start(f32[256,256]{1,0:T(8,128)S(1)} %bitcast.12), channel_id=1, source_target_pairs={{0,1},{1,2},{2,3},{3,0},{4,5},{5,6},{6,7},{7,4},{8,9},{9,10},{10,1... | collective-permute-start | bytes 786440 | tf_op jit(solution)/shard_map/ppermute | solution.py:200
  55.0 0.8 %labels.1.pi_ref = bf16[1024,256]{1,0:T(8,128)(2,1)S(1)} custom-call(s32[4]{0:T(128)S(1)} %copy-done.3, s32[16,16]{1,0:T(8,128)S(1)} %copy-done.1, s32[32]{0:T(128)S(1)} %copy-done.4, s32[32]{0:T(128)S(1)} %copy-done.5), custom_call_target="tpu_custom_call" | custom-call | flops 4000000 | bytes 1000000 | tf_op jit(solution)/shard_map/labels/pallas_call | solution.py:140
  55.8 0.8 %products_own.1.refs_4_ = f32[4,256,256]{2,1,0:T(8,128)S(1)} custom-call(bf16[1024,256]{1,0:T(8,128)(2,1)S(1)} %labels.1.pi_ref, f32[256,256]{1,0:T(8,128)S(1)} %bitcast.13, f32[4,256,256]{2,1,0:T(8,128)S(1)} %bitcast.8), custom_call_target="tpu_custom_call" | custom-call | flops 536870912 | bytes 2359296 | tf_op jit(solution)/shard_map/products_own/pallas_call | solution.py:181
  56.6 0.0 collective-permute-done.1.refs_0_
  56.6 2.3 %collective-permute-start.4 = (f32[256,256]{1,0:T(8,128)S(1)}, f32[256,256]{1,0:T(8,128)S(1)}, u32[]{:S(2)}, u32[]{:S(2)}) collective-permute-start(f32[256,256]{1,0:T(8,128)S(1)} %collective-permute-done.1.refs_0_), channel_id=1, source_target_pairs={{0,3},{1,0},{2,1},{3,2},{4,7},{5,4},{6,5},{7,6},{8,11},{9,8},{10,9... | collective-permute-start | bytes 786440 | tf_op jit(solution)/shard_map/ppermute | solution.py:207
  58.9 0.0 collective-permute-start.3
  58.9 1.6 %collective-permute-done.refs_1_ = f32[256,256]{1,0:T(8,128)S(1)} collective-permute-done((f32[256,256]{1,0:T(8,128)S(1)}, f32[256,256]{1,0:T(8,128)S(1)}, u32[]{:S(2)}, u32[]{:S(2)}) %collective-permute-start) | collective-permute-done | bytes 262176 | tf_op jit(solution)/shard_map/ppermute | solution.py:203
  60.5 1.0 %collective-permute-start.2 = (f32[256,256]{1,0:T(8,128)S(1)}, f32[256,256]{1,0:T(8,128)S(1)}, u32[]{:S(2)}, u32[]{:S(2)}) collective-permute-start(f32[256,256]{1,0:T(8,128)S(1)} %collective-permute-done.refs_1_), channel_id=1, source_target_pairs={{0,4},{1,5},{2,6},{3,7},{4,0},{5,1},{6,2},{7,3},{8,12},{9,13},{10,... | collective-permute-start | bytes 786440 | tf_op jit(solution)/shard_map/ppermute | solution.py:209
  61.5 5.0 %collective-permute-done.6.refs_3_ = f32[256,256]{1,0:T(8,128)S(1)} collective-permute-done((f32[256,256]{1,0:T(8,128)S(1)}, f32[256,256]{1,0:T(8,128)S(1)}, u32[]{:S(2)}, u32[]{:S(2)}) %collective-permute-start.6) | collective-permute-done | bytes 262176 | tf_op jit(solution)/shard_map/ppermute | solution.py:201
  66.5 0.0 collective-permute-done.5.refs_2_
  66.5 2.5 %products_near.1.refs_2_ = f32[4,256,256]{2,1,0:T(8,128)S(1)} custom-call(bf16[1024,256]{1,0:T(8,128)(2,1)S(1)} %labels.1.pi_ref, f32[256,256]{1,0:T(8,128)S(1)} %collective-permute-done.1.refs_0_, f32[256,256]{1,0:T(8,128)S(1)} %collective-permute-done.refs_1_, f32[256,256]{1,0:T(8,128)S(1)} %collective-permute-done.5.refs_2_, ...), custom_call_target="tpu_custom_call" | custom-call | flops 2147483648 | bytes 3145728 | tf_op jit(solution)/shard_map/products_near/pallas_call | solution.py:181
  69.0 0.8 %collective-permute-done.4.refs_1_ = f32[256,256]{1,0:T(8,128)S(1)} collective-permute-done((f32[256,256]{1,0:T(8,128)S(1)}, f32[256,256]{1,0:T(8,128)S(1)}, u32[]{:S(2)}, u32[]{:S(2)}) %collective-permute-start.4) | collective-permute-done | bytes 262176 | tf_op jit(solution)/shard_map/ppermute | solution.py:207
  69.8 0.0 collective-permute-done.3.refs_0_
  69.8 1.3 %products_beside.1.refs_1_ = f32[4,256,256]{2,1,0:T(8,128)S(1)} custom-call(bf16[1024,256]{1,0:T(8,128)(2,1)S(1)} %labels.1.pi_ref, f32[256,256]{1,0:T(8,128)S(1)} %collective-permute-done.3.refs_0_, f32[256,256]{1,0:T(8,128)S(1)} %collective-permute-done.4.refs_1_, f32[4,256,256]{2,1,0:T(8,128)S(1)} %products_near.1.refs_2_), custom_call_target="tpu_custom_call" | custom-call | flops 1073741824 | bytes 2621440 | tf_op jit(solution)/shard_map/products_beside/pallas_call | solution.py:181
  71.2 0.0 collective-permute-done.2.refs_0_
  71.2 1.6 %products_far.1 = f32[4,256,256]{2,1,0:T(8,128)} custom-call(bf16[1024,256]{1,0:T(8,128)(2,1)S(1)} %labels.1.pi_ref, f32[256,256]{1,0:T(8,128)S(1)} %collective-permute-done.2.refs_0_, f32[4,256,256]{2,1,0:T(8,128)S(1)} %products_beside.1.refs_1_), custom_call_target="tpu_custom_call" | custom-call | flops 536870912 | bytes 2359296 | tf_op jit(solution)/shard_map/products_far/pallas_call | solution.py:181
  (11 shorter events, 0.0 us)
Async XLA Ops:
  0.0 30.3 %copy-start.2 = (s32[1,32]{1,0:T(1,128)S(1)}, s32[1,32]{1,0:T(1,128)}, u32[]{:S(2)}) copy-start(s32[1,32]{1,0:T(1,128)} %targets_ref.1) | copy-start | bytes 388
  0.0 54.9 %copy-start.1 = (s32[16,16]{1,0:T(8,128)S(1)}, s32[16,16]{1,0:T(8,128)}, u32[]{:S(2)}) copy-start(s32[16,16]{1,0:T(8,128)} %ms_ref.1) | copy-start | bytes 3076
  0.0 54.9 %copy-start.3 = (s32[4]{0:T(128)S(1)}, s32[4]{0:T(128)}, u32[]{:S(2)}) copy-start(s32[4]{0:T(128)} %own_ref.1) | copy-start | bytes 52
  0.0 54.9 %copy-start.4 = (s32[32]{0:T(128)S(1)}, s32[32]{0:T(128)}, u32[]{:S(2)}) copy-start(s32[32]{0:T(128)} %tm_ref.1) | copy-start | bytes 388
  0.0 54.9 %copy-start.5 = (s32[32]{0:T(128)S(1)}, s32[32]{0:T(128)}, u32[]{:S(2)}) copy-start(s32[32]{0:T(128)} %tf_ref.1) | copy-start | bytes 388
  0.0 55.8 %copy-start = (f32[1,4,256,256]{3,2,1,0:T(8,128)S(1)}, f32[1,4,256,256]{3,2,1,0:T(8,128)}, u32[]{:S(2)}) copy-start(f32[1,4,256,256]{3,2,1,0:T(8,128)} %param.21) | copy-start | bytes 3145732
  47.0 9.6 %collective-permute-start.1 = (f32[256,256]{1,0:T(8,128)S(1)}, f32[256,256]{1,0:T(8,128)S(1)}, u32[]{:S(2)}, u32[]{:S(2)}) collective-permute-start(f32[256,256]{1,0:T(8,128)S(1)} %bitcast.9), channel_id=1, source_target_pairs={{0,4},{1,5},{2,6},{3,7},{4,0},{5,1},{6,2},{7,3},{8,12},{9,13},{10,... | collective-permute-start | bytes 786440 | tf_op jit(solution)/shard_map/ppermute | solution.py:202
  49.7 10.8 %collective-permute-start = (f32[256,256]{1,0:T(8,128)S(1)}, f32[256,256]{1,0:T(8,128)S(1)}, u32[]{:S(2)}, u32[]{:S(2)}) collective-permute-start(f32[256,256]{1,0:T(8,128)S(1)} %bitcast.10), channel_id=1, source_target_pairs={{0,2},{1,3},{2,0},{3,1},{4,6},{5,7},{6,4},{7,5},{8,10},{9,11},{10,... | collective-permute-start | bytes 786440 | tf_op jit(solution)/shard_map/ppermute | solution.py:203
  52.9 13.6 %collective-permute-start.6 = (f32[256,256]{1,0:T(8,128)S(1)}, f32[256,256]{1,0:T(8,128)S(1)}, u32[]{:S(2)}, u32[]{:S(2)}) collective-permute-start(f32[256,256]{1,0:T(8,128)S(1)} %bitcast.11), channel_id=1, source_target_pairs={{0,3},{1,0},{2,1},{3,2},{4,7},{5,4},{6,5},{7,6},{8,11},{9,8},{10,9... | collective-permute-start | bytes 786440 | tf_op jit(solution)/shard_map/ppermute | solution.py:201
  54.0 12.5 %collective-permute-start.5 = (f32[256,256]{1,0:T(8,128)S(1)}, f32[256,256]{1,0:T(8,128)S(1)}, u32[]{:S(2)}, u32[]{:S(2)}) collective-permute-start(f32[256,256]{1,0:T(8,128)S(1)} %bitcast.12), channel_id=1, source_target_pairs={{0,1},{1,2},{2,3},{3,0},{4,5},{5,6},{6,7},{7,4},{8,9},{9,10},{10,1... | collective-permute-start | bytes 786440 | tf_op jit(solution)/shard_map/ppermute | solution.py:200
  56.6 13.3 %collective-permute-start.4 = (f32[256,256]{1,0:T(8,128)S(1)}, f32[256,256]{1,0:T(8,128)S(1)}, u32[]{:S(2)}, u32[]{:S(2)}) collective-permute-start(f32[256,256]{1,0:T(8,128)S(1)} %collective-permute-done.1.refs_0_), channel_id=1, source_target_pairs={{0,3},{1,0},{2,1},{3,2},{4,7},{5,4},{6,5},{7,6},{8,11},{9,8},{10,9... | collective-permute-start | bytes 786440 | tf_op jit(solution)/shard_map/ppermute | solution.py:207
  58.9 10.9 %collective-permute-start.3 = (f32[256,256]{1,0:T(8,128)S(1)}, f32[256,256]{1,0:T(8,128)S(1)}, u32[]{:S(2)}, u32[]{:S(2)}) collective-permute-start(f32[256,256]{1,0:T(8,128)S(1)} %collective-permute-done.1.refs_0_), channel_id=1, source_target_pairs={{0,1},{1,2},{2,3},{3,0},{4,5},{5,6},{6,7},{7,4},{8,9},{9,10},{10,1... | collective-permute-start | bytes 786440 | tf_op jit(solution)/shard_map/ppermute | solution.py:206
  60.5 10.7 %collective-permute-start.2 = (f32[256,256]{1,0:T(8,128)S(1)}, f32[256,256]{1,0:T(8,128)S(1)}, u32[]{:S(2)}, u32[]{:S(2)}) collective-permute-start(f32[256,256]{1,0:T(8,128)S(1)} %collective-permute-done.refs_1_), channel_id=1, source_target_pairs={{0,4},{1,5},{2,6},{3,7},{4,0},{5,1},{6,2},{7,3},{8,12},{9,13},{10,... | collective-permute-start | bytes 786440 | tf_op jit(solution)/shard_map/ppermute | solution.py:209

commit v4 on v3

--- a/solution.py
+++ b/solution.py
@@ -13,7 +13,7 @@
 NW = 16
 NK = 16
 KW = 256
-M_CHUNKS = 2
+M_FIRST = 768
 F32 = jnp.float32
 BF16 = jnp.bfloat16
 
@@ -35,25 +35,23 @@
     return lax.dot_general(a, b, (((1,), (1,)), ((), ())), preferred_element_type=F32)
 
 
-def mm_split(hi, lo, b):
+def mm_split(hi, lo, b, product=mm):
     count = hi.shape[0]
-    both = mm(jnp.concatenate([hi, lo]), b)
+    both = product(jnp.concatenate([hi, lo]), b)
     return both[:count] + both[count:]
 
 
 def walker_kernel(m_hbm, u_hbm, rows_hbm, l_hbm, r_hbm, out_ref, m_v, u_v, rows_v, l_v, r_v, p_ref, s_ref, sems):
-    size = ORDER // M_CHUNKS
     copy_rows = pltpu.make_async_copy(rows_hbm, rows_v, sems.at[0])
     copy_l = pltpu.make_async_copy(l_hbm, l_v, sems.at[1])
     copy_r = pltpu.make_async_copy(r_hbm, r_v, sems.at[2])
     copy_u = [pltpu.make_async_copy(u_hbm.at[u], u_v.at[u], sems.at[3 + u]) for u in range(UPD)]
+    spans = [pl.ds(0, M_FIRST), pl.ds(M_FIRST, ORDER - M_FIRST)]
     copy_m = [
-        pltpu.make_async_copy(
-            m_hbm.at[pl.ds(k * size, size), :], m_v.at[pl.ds(k * size, size), :], sems.at[3 + UPD + k]
-        )
-        for k in range(M_CHUNKS)
+        pltpu.make_async_copy(m_hbm.at[span, :], m_v.at[span, :], sems.at[3 + UPD + k])
+        for k, span in enumerate(spans)
     ]
-    for copy in (copy_rows, copy_r, *copy_m, copy_l, copy_u[3], copy_u[0], copy_u[2], copy_u[1]):
+    for copy in (copy_rows, copy_r, *copy_m, copy_l, copy_u[3], copy_u[2], copy_u[0], copy_u[1]):
         copy.start()
 
     lane = lax.broadcasted_iota(jnp.int32, (RANK, ORDER), 1)
@@ -63,27 +61,29 @@
         s_ref[u] = jnp.where(lane == column, 1.0, 0.0).astype(BF16)
 
     copy_r.wait()
-    r_hi, r_lo = split(r_v[...])
-    for k in range(M_CHUNKS):
-        copy_m[k].wait()
-        m_hi, m_lo = split(m_v[pl.ds(k * size, size), :])
-        p_ref[pl.ds(k * size, size), :] = mm_split(m_hi, m_lo, r_hi) + mm(m_hi, r_lo)
-    copy_l.wait()
-    for copy in copy_u:
+    r_hi, r_lo = split(r_v[...].T)
+
+    def multiply(span):
+        m_hi, m_lo = split(m_v[span, :])
+        p_ref[:, span] = mm_split(r_hi, r_lo, m_hi, mm_nt) + mm_nt(r_hi, m_lo)
+
+    copy_m[0].wait()
+    multiply(spans[0])
+    for copy in (copy_m[1], copy_l, *copy_u):
         copy.wait()
+    left = l_v[...].T
+    multiply(spans[1])
     right = p_ref[...]
-    left = l_v[...].T
     for early, late in ((0, 3), (1, 2)):
         right_hi, right_lo = split(right)
-        picked_hi = mm(s_ref[early], right_hi).astype(BF16)
-        picked_lo = mm(s_ref[early], right_lo).astype(BF16)
-        right = right + (mm(u_v[early], picked_hi) + mm(u_v[early], picked_lo))
+        x_hi, x_lo = split(mm_split(right_hi, right_lo, s_ref[early], mm_nt))
+        right = right + mm_split(x_hi, x_lo, u_v[early], mm_nt)
         left_hi, left_lo = split(left)
         x_hi, x_lo = split(mm_split(left_hi, left_lo, u_v[late]))
         left = left + mm_split(x_hi, x_lo, s_ref[late])
     left_hi, left_lo = split(left)
     right_hi, right_lo = split(right)
-    out_ref[...] = mm_split(left_hi, left_lo, right_hi) + mm(left_hi, right_lo)
+    out_ref[...] = mm_split(left_hi, left_lo, right_hi, mm_nt) + mm_nt(left_hi, right_lo)
 
 
 def walker(matrix, updates, rows, left, right):
@@ -98,9 +98,9 @@
             pltpu.VMEM((UPD, RANK), jnp.int32),
             pltpu.VMEM((ORDER, KW), F32),
             pltpu.VMEM((ORDER, KW), F32),
-            pltpu.VMEM((ORDER, KW), F32),
+            pltpu.VMEM((KW, ORDER), F32),
             pltpu.VMEM((UPD, RANK, ORDER), BF16),
-            pltpu.SemaphoreType.DMA((3 + UPD + M_CHUNKS,)),
+            pltpu.SemaphoreType.DMA((5 + UPD,)),
         ],
         compiler_params=pltpu.CompilerParams(vmem_limit_bytes=24 << 20),
         name="walker",
@@ -197,19 +197,19 @@
     upward = [(j, j // 4 * 4 + (j % 4 + 1) % 4) for j in range(8)]
     downward = [(j, j // 4 * 4 + (j % 4 + 3) % 4) for j in range(8)]
     opposite = [(j, j // 4 * 4 + (j % 4 + 2) % 4) for j in range(8)]
+    far = lax.ppermute(own, "blk", opposite)
+    beside = lax.ppermute(own, "blk", across)
     below = lax.ppermute(own, "blk", upward)
     above = lax.ppermute(own, "blk", downward)
-    beside = lax.ppermute(own, "blk", across)
-    far = lax.ppermute(own, "blk", opposite)
     total = products(scale, pi, [own], prior, "products_own")
+    far, total = lax.optimization_barrier((far, total))
+    beside_far = lax.ppermute(far, "blk", across)
     beside, total = lax.optimization_barrier((beside, total))
     beside_below = lax.ppermute(beside, "blk", upward)
     beside_above = lax.ppermute(beside, "blk", downward)
-    far, total = lax.optimization_barrier((far, total))
-    beside_far = lax.ppermute(far, "blk", across)
     total = products(scale, pi, [beside, far, below, above], total, "products_near")
-    total = products(scale, pi, [beside_below, beside_above], total, "products_beside")
-    return products(scale, pi, [beside_far], total, "products_far", last=True)
+    total = products(scale, pi, [beside_far], total, "products_far")
+    return products(scale, pi, [beside_below, beside_above], total, "products_last", last=True)
 
 
 def shards(

time: 74.2 us -> 72.7 us (0.980); the launches traced: 73 us -> 72.6 us
  starting transfers between devices: 11.3 us -> 14.8 us
  waiting for transfers between devices: 7.36 us -> 4.46 us
  Pallas kernels: 16.3 us -> 15.3 us
    ppermute x1, waiting for transfers between devices: 4.95 us -> 0.17 us  [cycle_products(): above = lax.ppermute(own, 'blk', downward)]
    ppermute x1, waiting for transfers between devices: 0.01 us -> 3.69 us  [cycle_products(): beside_below = lax.ppermute(beside, 'blk', upward)]
    ppermute x1, starting transfers between devices: 1.04 us -> 3.75 us  [cycle_products(): beside_far = lax.ppermute(far, 'blk', across)]
    ppermute x1, waiting for transfers between devices: 1.56 us -> 0.17 us  [cycle_products(): far = lax.ppermute(own, 'blk', opposite)]
    pallas_call x1, Pallas kernels: 8.62 us -> 7.71 us  [walker(): pl.pallas_call(walker_kernel, out_shape=jax.ShapeDtypeStruct((KW, KW), F3...]
  transfers between devices with their start and end apart: 7 -> 7, of which waited for: 3 -> 4; matrix products, arithmetic and copies ran while one was open for 0% -> 0% of each run, Pallas kernels for 7% -> 7%
where the time goes in v4:
time: 72.7 us; the launch traced here: 72.6 us
  blocking collectives  37.7 us (52%)
  Pallas kernels  15.3 us (21%)
  starting transfers between devices  14.8 us (20%)
  waiting for transfers between devices  4.46 us (6%)
    all_to_all x1, blocking collectives, shards(): lax.all_to_all(greens.reshape(n_grp, KW // n_grp, KW), 'grp', 0, 0, tiled...  21.6 us
    all_to_all x1, blocking collectives, shards(): measured = lax.all_to_all(routed, 'grp', 0, 0, tiled=True).reshape(KW, KW)  16.2 us
    pallas_call x1, Pallas kernels, walker(): pl.pallas_call(walker_kernel, out_shape=jax.ShapeDtypeStruct((KW, KW), F3...  7.71 us
    pallas_call x4, Pallas kernels, products(): pl.pallas_call(functools.partial(products_kernel, scale, last), out_shape...  6.21 us
    ppermute x1, starting transfers between devices, cycle_products(): beside_far = lax.ppermute(far, 'blk', across)  3.75 us
    ppermute x1, waiting for transfers between devices, cycle_products(): beside_below = lax.ppermute(beside, 'blk', upward)  3.69 us
    ppermute x1, starting transfers between devices, cycle_products(): far = lax.ppermute(own, 'blk', opposite)  3.2 us
    ppermute x1, starting transfers between devices, cycle_products(): beside_above = lax.ppermute(beside, 'blk', downward)  3.05 us
  transfers between devices with their start and end apart: 7, of which 4 were waited for; matrix products, arithmetic and copies ran while one was open for 0% of the time, Pallas kernels for 7%

profile of v4, /device:TPU:32, one launch (start us, length us, event | category | flops | bytes accessed | tf_op | source)
XLA Modules:
  0.0 72.6 jit_solution(9295854311485183042)
XLA Ops:
  0.0 7.7 %walker.1 = f32[256,256]{1,0:T(8,128)S(1)} custom-call(f32[1024,1024]{1,0:T(8,128)} %bitcast.14, bf16[4,1024,256]{2,1,0:T(8,128)(2,1)} %bitcast.15, s32[4,256]{1,0:T(4,128)} %bitcast.16, f32[1024,256]{1,0:T(8,128)} %l_hbm.1, f32[1024,256]{1,0:T(8,128)} %r_hbm.1), custom_call_target="tpu_custom_call" | custom-call | tf_op jit(solution)/shard_map/walker/pallas_call | solution.py:90
  7.8 21.6 %all_to_all.10.x_ref = f32[32,8,256]{2,1,0:T(8,128)S(1)} all-to-all(f32[32,8,256]{2,1,0:T(8,128)S(1)} %bitcast.7), channel_id=1, replica_groups=mesh['grp'=32,'blk'=8] {'grp'}, dimensions={0} | all-to-all | bytes 524288 | tf_op jit(solution)/shard_map/all_to_all | solution.py:222
  29.3 0.6 route.1
  29.9 16.2 %all_to_all.11 = f32[32,8,256]{2,1,0:T(8,128)S(1)} all-to-all(f32[32,8,256]{2,1,0:T(8,128)S(1)} %route.1), channel_id=1, replica_groups=mesh['grp'=32,'blk'=8] {'grp'}, dimensions={0} | all-to-all | bytes 524288 | tf_op jit(solution)/shard_map/all_to_all | solution.py:224
  46.1 3.2 %collective-permute-start.1 = (f32[256,256]{1,0:T(8,128)S(1)}, f32[256,256]{1,0:T(8,128)S(1)}, u32[]{:S(2)}, u32[]{:S(2)}) collective-permute-start(f32[256,256]{1,0:T(8,128)S(1)} %bitcast.9), channel_id=1, source_target_pairs={{0,2},{1,3},{2,0},{3,1},{4,6},{5,7},{6,4},{7,5},{8,10},{9,11},{10,... | collective-permute-start | bytes 786440 | tf_op jit(solution)/shard_map/ppermute | solution.py:200
  49.3 2.7 %collective-permute-start = (f32[256,256]{1,0:T(8,128)S(1)}, f32[256,256]{1,0:T(8,128)S(1)}, u32[]{:S(2)}, u32[]{:S(2)}) collective-permute-start(f32[256,256]{1,0:T(8,128)S(1)} %bitcast.10), channel_id=1, source_target_pairs={{0,4},{1,5},{2,6},{3,7},{4,0},{5,1},{6,2},{7,3},{8,12},{9,13},{10,... | collective-permute-start | bytes 786440 | tf_op jit(solution)/shard_map/ppermute | solution.py:201
  52.0 1.1 %collective-permute-start.6 = (f32[256,256]{1,0:T(8,128)S(1)}, f32[256,256]{1,0:T(8,128)S(1)}, u32[]{:S(2)}, u32[]{:S(2)}) collective-permute-start(f32[256,256]{1,0:T(8,128)S(1)} %bitcast.11), channel_id=1, source_target_pairs={{0,3},{1,0},{2,1},{3,2},{4,7},{5,4},{6,5},{7,6},{8,11},{9,8},{10,9... | collective-permute-start | bytes 786440 | tf_op jit(solution)/shard_map/ppermute | solution.py:203
  53.1 1.0 %collective-permute-start.5 = (f32[256,256]{1,0:T(8,128)S(1)}, f32[256,256]{1,0:T(8,128)S(1)}, u32[]{:S(2)}, u32[]{:S(2)}) collective-permute-start(f32[256,256]{1,0:T(8,128)S(1)} %bitcast.12), channel_id=1, source_target_pairs={{0,1},{1,2},{2,3},{3,0},{4,5},{5,6},{6,7},{7,4},{8,9},{9,10},{10,1... | collective-permute-start | bytes 786440 | tf_op jit(solution)/shard_map/ppermute | solution.py:202
  54.0 0.0 copy-done.3
  54.0 0.8 %labels.1.pi_ref = bf16[1024,256]{1,0:T(8,128)(2,1)S(1)} custom-call(s32[4]{0:T(128)S(1)} %copy-done.3, s32[16,16]{1,0:T(8,128)S(1)} %copy-done.1, s32[32]{0:T(128)S(1)} %copy-done.4, s32[32]{0:T(128)S(1)} %copy-done.5), custom_call_target="tpu_custom_call" | custom-call | flops 4000000 | bytes 1000000 | tf_op jit(solution)/shard_map/labels/pallas_call | solution.py:140
  54.9 0.8 %products_own.1.refs_4_ = f32[4,256,256]{2,1,0:T(8,128)S(1)} custom-call(bf16[1024,256]{1,0:T(8,128)(2,1)S(1)} %labels.1.pi_ref, f32[256,256]{1,0:T(8,128)S(1)} %bitcast.13, f32[4,256,256]{2,1,0:T(8,128)S(1)} %bitcast.8), custom_call_target="tpu_custom_call" | custom-call | flops 536870912 | bytes 2359296 | tf_op jit(solution)/shard_map/products_own/pallas_call | solution.py:181
  55.6 0.2 collective-permute-done.1.refs_1_
  55.8 3.8 %collective-permute-start.4 = (f32[256,256]{1,0:T(8,128)S(1)}, f32[256,256]{1,0:T(8,128)S(1)}, u32[]{:S(2)}, u32[]{:S(2)}) collective-permute-start(f32[256,256]{1,0:T(8,128)S(1)} %collective-permute-done.1.refs_1_), channel_id=1, source_target_pairs={{0,4},{1,5},{2,6},{3,7},{4,0},{5,1},{6,2},{7,3},{8,12},{9,13},{10,... | collective-permute-start | bytes 786440 | tf_op jit(solution)/shard_map/ppermute | solution.py:206
  59.6 0.0 collective-permute-done.refs_0_
  59.6 3.0 %collective-permute-start.3 = (f32[256,256]{1,0:T(8,128)S(1)}, f32[256,256]{1,0:T(8,128)S(1)}, u32[]{:S(2)}, u32[]{:S(2)}) collective-permute-start(f32[256,256]{1,0:T(8,128)S(1)} %collective-permute-done.refs_0_), channel_id=1, source_target_pairs={{0,3},{1,0},{2,1},{3,2},{4,7},{5,4},{6,5},{7,6},{8,11},{9,8},{10,9... | collective-permute-start | bytes 786440 | tf_op jit(solution)/shard_map/ppermute | solution.py:209
  62.6 0.0 collective-permute-start.2
  62.6 0.2 collective-permute-done.6.refs_3_
  62.8 0.0 collective-permute-done.5.refs_2_
  62.8 2.5 %products_near.1.refs_1_ = f32[4,256,256]{2,1,0:T(8,128)S(1)} custom-call(bf16[1024,256]{1,0:T(8,128)(2,1)S(1)} %labels.1.pi_ref, f32[256,256]{1,0:T(8,128)S(1)} %collective-permute-done.refs_0_, f32[256,256]{1,0:T(8,128)S(1)} %collective-permute-done.1.refs_1_, f32[256,256]{1,0:T(8,128)S(1)} %collective-permute-done.5.refs_2_, ...), custom_call_target="tpu_custom_call" | custom-call | flops 2147483648 | bytes 3145728 | tf_op jit(solution)/shard_map/products_near/pallas_call | solution.py:181
  65.3 0.0 collective-permute-done.4.refs_0_
  65.3 0.8 %products_far.1.refs_2_ = f32[4,256,256]{2,1,0:T(8,128)S(1)} custom-call(bf16[1024,256]{1,0:T(8,128)(2,1)S(1)} %labels.1.pi_ref, f32[256,256]{1,0:T(8,128)S(1)} %collective-permute-done.4.refs_0_, f32[4,256,256]{2,1,0:T(8,128)S(1)} %products_near.1.refs_1_), custom_call_target="tpu_custom_call" | custom-call | flops 536870912 | bytes 2359296 | tf_op jit(solution)/shard_map/products_far/pallas_call | solution.py:181
  66.1 0.4 collective-permute-done.3.refs_1_
  66.5 3.7 %collective-permute-done.2.refs_0_ = f32[256,256]{1,0:T(8,128)S(1)} collective-permute-done((f32[256,256]{1,0:T(8,128)S(1)}, f32[256,256]{1,0:T(8,128)S(1)}, u32[]{:S(2)}, u32[]{:S(2)}) %collective-permute-start.2) | collective-permute-done | bytes 262176 | tf_op jit(solution)/shard_map/ppermute | solution.py:208
  70.2 2.2 %products_last.1 = f32[4,256,256]{2,1,0:T(8,128)} custom-call(bf16[1024,256]{1,0:T(8,128)(2,1)S(1)} %labels.1.pi_ref, f32[256,256]{1,0:T(8,128)S(1)} %collective-permute-done.2.refs_0_, f32[256,256]{1,0:T(8,128)S(1)} %collective-permute-done.3.refs_1_, f32[4,256,256]{2,1,0:T(8,128)S(1)} %products_far.1.refs_2_), custom_call_target="tpu_custom_call" | custom-call | flops 1073741824 | bytes 2621440 | tf_op jit(solution)/shard_map/products_last/pallas_call | solution.py:181
  (11 shorter events, 0.0 us)
Async XLA Ops:
  0.0 29.3 %copy-start.2 = (s32[1,32]{1,0:T(1,128)S(1)}, s32[1,32]{1,0:T(1,128)}, u32[]{:S(2)}) copy-start(s32[1,32]{1,0:T(1,128)} %targets_ref.1) | copy-start | bytes 388
  0.0 54.0 %copy-start.1 = (s32[16,16]{1,0:T(8,128)S(1)}, s32[16,16]{1,0:T(8,128)}, u32[]{:S(2)}) copy-start(s32[16,16]{1,0:T(8,128)} %ms_ref.1) | copy-start | bytes 3076
  0.0 54.0 %copy-start.3 = (s32[4]{0:T(128)S(1)}, s32[4]{0:T(128)}, u32[]{:S(2)}) copy-start(s32[4]{0:T(128)} %own_ref.1) | copy-start | bytes 52
  0.0 54.0 %copy-start.4 = (s32[32]{0:T(128)S(1)}, s32[32]{0:T(128)}, u32[]{:S(2)}) copy-start(s32[32]{0:T(128)} %tm_ref.1) | copy-start | bytes 388
  0.0 54.0 %copy-start.5 = (s32[32]{0:T(128)S(1)}, s32[32]{0:T(128)}, u32[]{:S(2)}) copy-start(s32[32]{0:T(128)} %tf_ref.1) | copy-start | bytes 388
  0.0 54.8 %copy-start = (f32[1,4,256,256]{3,2,1,0:T(8,128)S(1)}, f32[1,4,256,256]{3,2,1,0:T(8,128)}, u32[]{:S(2)}) copy-start(f32[1,4,256,256]{3,2,1,0:T(8,128)} %param.21) | copy-start | bytes 3145732
  46.1 9.7 %collective-permute-start.1 = (f32[256,256]{1,0:T(8,128)S(1)}, f32[256,256]{1,0:T(8,128)S(1)}, u32[]{:S(2)}, u32[]{:S(2)}) collective-permute-start(f32[256,256]{1,0:T(8,128)S(1)} %bitcast.9), channel_id=1, source_target_pairs={{0,2},{1,3},{2,0},{3,1},{4,6},{5,7},{6,4},{7,5},{8,10},{9,11},{10,... | collective-permute-start | bytes 786440 | tf_op jit(solution)/shard_map/ppermute | solution.py:200
  49.3 10.3 %collective-permute-start = (f32[256,256]{1,0:T(8,128)S(1)}, f32[256,256]{1,0:T(8,128)S(1)}, u32[]{:S(2)}, u32[]{:S(2)}) collective-permute-start(f32[256,256]{1,0:T(8,128)S(1)} %bitcast.10), channel_id=1, source_target_pairs={{0,4},{1,5},{2,6},{3,7},{4,0},{5,1},{6,2},{7,3},{8,12},{9,13},{10,... | collective-permute-start | bytes 786440 | tf_op jit(solution)/shard_map/ppermute | solution.py:201
  52.0 10.8 %collective-permute-start.6 = (f32[256,256]{1,0:T(8,128)S(1)}, f32[256,256]{1,0:T(8,128)S(1)}, u32[]{:S(2)}, u32[]{:S(2)}) collective-permute-start(f32[256,256]{1,0:T(8,128)S(1)} %bitcast.11), channel_id=1, source_target_pairs={{0,3},{1,0},{2,1},{3,2},{4,7},{5,4},{6,5},{7,6},{8,11},{9,8},{10,9... | collective-permute-start | bytes 786440 | tf_op jit(solution)/shard_map/ppermute | solution.py:203
  53.1 9.7 %collective-permute-start.5 = (f32[256,256]{1,0:T(8,128)S(1)}, f32[256,256]{1,0:T(8,128)S(1)}, u32[]{:S(2)}, u32[]{:S(2)}) collective-permute-start(f32[256,256]{1,0:T(8,128)S(1)} %bitcast.12), channel_id=1, source_target_pairs={{0,1},{1,2},{2,3},{3,0},{4,5},{5,6},{6,7},{7,4},{8,9},{9,10},{10,1... | collective-permute-start | bytes 786440 | tf_op jit(solution)/shard_map/ppermute | solution.py:202
  55.8 9.5 %collective-permute-start.4 = (f32[256,256]{1,0:T(8,128)S(1)}, f32[256,256]{1,0:T(8,128)S(1)}, u32[]{:S(2)}, u32[]{:S(2)}) collective-permute-start(f32[256,256]{1,0:T(8,128)S(1)} %collective-permute-done.1.refs_1_), channel_id=1, source_target_pairs={{0,4},{1,5},{2,6},{3,7},{4,0},{5,1},{6,2},{7,3},{8,12},{9,13},{10,... | collective-permute-start | bytes 786440 | tf_op jit(solution)/shard_map/ppermute | solution.py:206
  59.6 6.9 %collective-permute-start.3 = (f32[256,256]{1,0:T(8,128)S(1)}, f32[256,256]{1,0:T(8,128)S(1)}, u32[]{:S(2)}, u32[]{:S(2)}) collective-permute-start(f32[256,256]{1,0:T(8,128)S(1)} %collective-permute-done.refs_0_), channel_id=1, source_target_pairs={{0,3},{1,0},{2,1},{3,2},{4,7},{5,4},{6,5},{7,6},{8,11},{9,8},{10,9... | collective-permute-start | bytes 786440 | tf_op jit(solution)/shard_map/ppermute | solution.py:209
  62.6 7.6 %collective-permute-start.2 = (f32[256,256]{1,0:T(8,128)S(1)}, f32[256,256]{1,0:T(8,128)S(1)}, u32[]{:S(2)}, u32[]{:S(2)}) collective-permute-start(f32[256,256]{1,0:T(8,128)S(1)} %collective-permute-done.refs_0_), channel_id=1, source_target_pairs={{0,1},{1,2},{2,3},{3,0},{4,5},{5,6},{6,7},{7,4},{8,9},{9,10},{10,1... | collective-permute-start | bytes 786440 | tf_op jit(solution)/shard_map/ppermute | solution.py:208

commit v5 on v4

--- a/solution.py
+++ b/solution.py
@@ -107,20 +107,38 @@
     )(*(pltpu.with_memory_space_constraint(x, pltpu.HBM) for x in (matrix, updates, rows, left, right)))
 
 
-def route_kernel(n, targets_ref, x_ref, out_ref):
-    for w in range(n):
-        out_ref[targets_ref[0, w]] = x_ref[w]
-
-
-def route(targets, chunks):
-    return pl.pallas_call(
-        functools.partial(route_kernel, chunks.shape[0]),
-        out_shape=jax.ShapeDtypeStruct(chunks.shape, F32),
-        in_specs=[SMEM, VMEM],
+def route_kernel(core_ref, targets_ref, own_ref, other_ref, out_ref):
+    core = core_ref[0]
+    for pair in range(own_ref.shape[0]):
+        for part, source_ref in ((core, own_ref), (1 - core, other_ref)):
+            target = targets_ref[0, 2 * pair + part]
+
+            @pl.when((target & 1) == core)
+            def _():
+                out_ref[target >> 1] = source_ref[pair]
+
+
+def route(core, targets, own, other):
+    return pl.pallas_call(
+        route_kernel,
+        out_shape=jax.ShapeDtypeStruct(own.shape, F32),
+        in_specs=[SMEM, SMEM, VMEM, VMEM],
         out_specs=VMEM,
         compiler_params=pltpu.CompilerParams(vmem_limit_bytes=8 << 20),
         name="route",
-    )(targets, chunks)
+    )(core, targets, own, other)
+
+
+def permute_walkers(greens, targets):
+    n_grp = lax.axis_size("grp")
+    pairs = n_grp // 2
+    core = lax.axis_index("grp") & 1
+    alike = [[2 * pair + part for pair in range(pairs)] for part in range(2)]
+    chunks = greens.reshape(pairs, KW // pairs, KW)
+    own = lax.all_to_all(chunks, "grp", 0, 0, axis_index_groups=alike, tiled=True)
+    other = lax.ppermute(own, "grp", [(w, w ^ 1) for w in range(n_grp)])
+    routed = route(core.reshape(1), targets, own, other)
+    return lax.all_to_all(routed, "grp", 0, 0, axis_index_groups=alike, tiled=True).reshape(KW, KW)
 
 
 def labels_kernel(own_ref, ms_ref, tm_ref, tf_ref, pi_ref):
@@ -155,24 +173,23 @@
         *piece_refs, total_ref, out_ref = refs
     held = total_ref.shape[0]
     pi = pi_ref[...]
-    terms = [total_ref[j] for j in range(held)]
-    for number, piece_ref in enumerate(piece_refs):
-        a = piece_ref[...]
-        a_hi, a_lo = split(a)
-        v_hi = mm_nt(pi, a_hi).astype(BF16)
-        v_lo = mm_nt(pi, a_lo).astype(BF16)
-        a = a * scale
+    blocks = []
+    for piece_ref in piece_refs:
+        a_hi, a_lo = split(piece_ref[...])
+        blocks.append((mm_nt(pi, a_hi).astype(BF16), mm_nt(pi, a_lo).astype(BF16)))
+    for j in range(held):
+        rows = slice(j * KW, (j + 1) * KW)
+        term = total_ref[j]
+        for piece_ref, (v_hi, v_lo) in zip(piece_refs, blocks):
+            term += piece_ref[...] * scale * (mm_nt(v_hi[rows], pi[rows]) + mm_nt(v_lo[rows], pi[rows]))
+        if last:
+            out_v[j] = term
+            pltpu.make_async_copy(out_v.at[j], out_hbm.at[j], sems.at[j]).start()
+        else:
+            out_ref[j] = term
+    if last:
         for j in range(held):
-            rows = slice(j * KW, (j + 1) * KW)
-            terms[j] += a * (mm_nt(v_hi[rows], pi[rows]) + mm_nt(v_lo[rows], pi[rows]))
-            if last and number == len(piece_refs) - 1:
-                out_v[j] = terms[j]
-                pltpu.make_async_copy(out_v.at[j], out_hbm.at[j], sems.at[j]).start()
-    for j in range(held):
-        if last:
             pltpu.make_async_copy(out_v.at[j], out_hbm.at[j], sems.at[j]).wait()
-        else:
-            out_ref[j] = terms[j]
 
 
 def products(scale, pi, pieces, total, name, last=False):
@@ -216,12 +233,9 @@
     walker_matrix, updates, update_rows, left_table, right_table, assignment, momentum_sum,
     transfer_momentum, transfer_frequency, ownership, g4_prior,
 ):
-    n_grp = lax.axis_size("grp")
     pi = labels(ownership, momentum_sum, transfer_momentum, transfer_frequency)
     greens = walker(walker_matrix[0, 0], updates[0, 0], update_rows[0, 0], left_table, right_table)
-    chunks = lax.all_to_all(greens.reshape(n_grp, KW // n_grp, KW), "grp", 0, 0, tiled=True)
-    routed = route(assignment, chunks)
-    measured = lax.all_to_all(routed, "grp", 0, 0, tiled=True).reshape(KW, KW)
+    measured = permute_walkers(greens, assignment)
     scale = 1.0 / lax.axis_size("blk")
     return cycle_products(scale, pi, measured, g4_prior[0])[None]
 

time: 72.7 us -> 70.7 us (0.972)
  blocking collectives: 37.7 us -> 34.1 us
  waiting for transfers between devices: 4.46 us -> 5.95 us
    all_to_all x2, blocking collectives: 37.7 us -> 34.1 us  [the longest x1 19.4 us: permute_walkers(): lax.all_to_all(chunks, 'grp', 0, 0, axis_index_groups=alike, tiled=True)]
    ppermute x0 -> x1, waiting for transfers between devices: none -> 1.53 us  [permute_walkers(): other = lax.ppermute(own, 'grp', [(w, w ^ 1) for w in range(n_grp)])]
  transfers between devices with their start and end apart: 7 -> 8, of which waited for: 4 -> 3; matrix products, arithmetic and copies ran while one was open for 0% -> 0% of each run, Pallas kernels for 7% -> 7%
where the time goes in v5:
time: 70.7 us; the launch traced here: 70.5 us
  blocking collectives  34.1 us (48%)
  Pallas kernels  15.3 us (22%)
  starting transfers between devices  14.9 us (21%)
  waiting for transfers between devices  5.95 us (8%)
    all_to_all x1, blocking collectives, permute_walkers(): lax.all_to_all(chunks, 'grp', 0, 0, axis_index_groups=alike, tiled=True)  19.4 us
    all_to_all x1, blocking collectives, permute_walkers(): lax.all_to_all(routed, 'grp', 0, 0, axis_index_groups=alike, tiled=True)  14.7 us
    pallas_call x1, Pallas kernels, walker(): pl.pallas_call(walker_kernel, out_shape=jax.ShapeDtypeStruct((KW, KW), F3...  7.71 us
    pallas_call x4, Pallas kernels, products(): pl.pallas_call(functools.partial(products_kernel, scale, last), out_shape...  5.93 us
    ppermute x1, starting transfers between devices, cycle_products(): beside_far = lax.ppermute(far, 'blk', across)  3.91 us
    ppermute x1, waiting for transfers between devices, cycle_products(): beside_below = lax.ppermute(beside, 'blk', upward)  3.69 us
    ppermute x1, starting transfers between devices, cycle_products(): far = lax.ppermute(own, 'blk', opposite)  3.19 us
    ppermute x1, starting transfers between devices, cycle_products(): beside_above = lax.ppermute(beside, 'blk', downward)  3.06 us
  transfers between devices with their start and end apart: 8, of which 3 were waited for; matrix products, arithmetic and copies ran while one was open for 0% of the time, Pallas kernels for 7%

profile of v5, /device:TPU:32, one launch (start us, length us, event | category | flops | bytes accessed | tf_op | source)
XLA Modules:
  0.0 70.5 jit_solution(10645965892952407264)
XLA Ops:
  0.0 7.7 %walker.1 = f32[256,256]{1,0:T(8,128)S(1)} custom-call(f32[1024,1024]{1,0:T(8,128)} %bitcast.15, bf16[4,1024,256]{2,1,0:T(8,128)(2,1)} %bitcast.16, s32[4,256]{1,0:T(4,128)} %bitcast.17, f32[1024,256]{1,0:T(8,128)} %l_hbm.1, f32[1024,256]{1,0:T(8,128)} %r_hbm.1), custom_call_target="tpu_custom_call" | custom-call | tf_op jit(solution)/shard_map/walker/pallas_call | solution.py:90
  7.8 19.4 %all_to_all.10.own_ref = f32[16,16,256]{2,1,0:T(8,128)S(1)} all-to-all(f32[16,16,256]{2,1,0:T(8,128)S(1)} %bitcast.8), channel_id=1, replica_groups={{0,16,32,48,64,80,96,112,128,144,160,176,192,208,224,240},{8,24,40,56,7..., dimensions={0} | all-to-all | bytes 524288 | tf_op jit(solution)/shard_map/all_to_all | solution.py:138
  27.1 0.0 collective-permute-start
  27.1 1.5 %collective-permute-done.other_ref = f32[16,16,256]{2,1,0:T(8,128)S(1)} collective-permute-done((f32[16,16,256]{2,1,0:T(8,128)S(1)}, f32[16,16,256]{2,1,0:T(8,128)S(1)}, u32[]{:S(2)}, u32[]{:S(2)}) %collective-permute-start) | collective-permute-done | bytes 262176 | tf_op jit(solution)/shard_map/ppermute | solution.py:139
  28.7 0.8 %route.1 = f32[16,16,256]{2,1,0:T(8,128)S(1)} custom-call(s32[1]{0:T(128)} %bitcast.core_ref, s32[1,32]{1,0:T(1,128)S(1)} %copy-done.2, f32[16,16,256]{2,1,0:T(8,128)S(1)} %all_to_all.10.own_ref, f32[16,16,256]{2,1,0:T(8,128)S(1)} %collective-permute-done.other_ref), custom_call_target="tpu_custom_call" | custom-call | tf_op jit(solution)/shard_map/route/pallas_call | solution.py:122
  29.5 14.7 %all_to_all.11 = f32[16,16,256]{2,1,0:T(8,128)S(1)} all-to-all(f32[16,16,256]{2,1,0:T(8,128)S(1)} %route.1), channel_id=1, replica_groups={{0,16,32,48,64,80,96,112,128,144,160,176,192,208,224,240},{8,24,40,56,7..., dimensions={0} | all-to-all | bytes 524288 | tf_op jit(solution)/shard_map/all_to_all | solution.py:141
  44.2 3.2 %collective-permute-start.2 = (f32[256,256]{1,0:T(8,128)S(1)}, f32[256,256]{1,0:T(8,128)S(1)}, u32[]{:S(2)}, u32[]{:S(2)}) collective-permute-start(f32[256,256]{1,0:T(8,128)S(1)} %bitcast.10), channel_id=1, source_target_pairs={{0,2},{1,3},{2,0},{3,1},{4,6},{5,7},{6,4},{7,5},{8,10},{9,11},{10,... | collective-permute-start | bytes 786440 | tf_op jit(solution)/shard_map/ppermute | solution.py:217
  47.4 2.7 %collective-permute-start.1 = (f32[256,256]{1,0:T(8,128)S(1)}, f32[256,256]{1,0:T(8,128)S(1)}, u32[]{:S(2)}, u32[]{:S(2)}) collective-permute-start(f32[256,256]{1,0:T(8,128)S(1)} %bitcast.11), channel_id=1, source_target_pairs={{0,4},{1,5},{2,6},{3,7},{4,0},{5,1},{6,2},{7,3},{8,12},{9,13},{10,... | collective-permute-start | bytes 786440 | tf_op jit(solution)/shard_map/ppermute | solution.py:218
  50.1 1.1 %collective-permute-start.7 = (f32[256,256]{1,0:T(8,128)S(1)}, f32[256,256]{1,0:T(8,128)S(1)}, u32[]{:S(2)}, u32[]{:S(2)}) collective-permute-start(f32[256,256]{1,0:T(8,128)S(1)} %bitcast.12), channel_id=1, source_target_pairs={{0,3},{1,0},{2,1},{3,2},{4,7},{5,4},{6,5},{7,6},{8,11},{9,8},{10,9... | collective-permute-start | bytes 786440 | tf_op jit(solution)/shard_map/ppermute | solution.py:220
  51.2 1.0 %collective-permute-start.6 = (f32[256,256]{1,0:T(8,128)S(1)}, f32[256,256]{1,0:T(8,128)S(1)}, u32[]{:S(2)}, u32[]{:S(2)}) collective-permute-start(f32[256,256]{1,0:T(8,128)S(1)} %bitcast.13), channel_id=1, source_target_pairs={{0,1},{1,2},{2,3},{3,0},{4,5},{5,6},{6,7},{7,4},{8,9},{9,10},{10,1... | collective-permute-start | bytes 786440 | tf_op jit(solution)/shard_map/ppermute | solution.py:219
  52.2 0.8 %labels.1.pi_ref = bf16[1024,256]{1,0:T(8,128)(2,1)S(1)} custom-call(s32[4]{0:T(128)S(1)} %copy-done.3, s32[16,16]{1,0:T(8,128)S(1)} %copy-done.1, s32[32]{0:T(128)S(1)} %copy-done.4, s32[32]{0:T(128)S(1)} %copy-done.5), custom_call_target="tpu_custom_call" | custom-call | flops 4000000 | bytes 1000000 | tf_op jit(solution)/shard_map/labels/pallas_call | solution.py:158
  53.0 0.7 %products_own.1.refs_4_ = f32[4,256,256]{2,1,0:T(8,128)S(1)} custom-call(bf16[1024,256]{1,0:T(8,128)(2,1)S(1)} %labels.1.pi_ref, f32[256,256]{1,0:T(8,128)S(1)} %bitcast.14, f32[4,256,256]{2,1,0:T(8,128)S(1)} %bitcast.9), custom_call_target="tpu_custom_call" | custom-call | flops 536870912 | bytes 2359296 | tf_op jit(solution)/shard_map/products_own/pallas_call | solution.py:198
  53.8 0.0 collective-permute-done.2.refs_1_
  53.8 3.9 %collective-permute-start.5 = (f32[256,256]{1,0:T(8,128)S(1)}, f32[256,256]{1,0:T(8,128)S(1)}, u32[]{:S(2)}, u32[]{:S(2)}) collective-permute-start(f32[256,256]{1,0:T(8,128)S(1)} %collective-permute-done.2.refs_1_), channel_id=1, source_target_pairs={{0,4},{1,5},{2,6},{3,7},{4,0},{5,1},{6,2},{7,3},{8,12},{9,13},{10,... | collective-permute-start | bytes 786440 | tf_op jit(solution)/shard_map/ppermute | solution.py:223
  57.7 0.0 collective-permute-done.1.refs_0_
  57.7 3.1 %collective-permute-start.4 = (f32[256,256]{1,0:T(8,128)S(1)}, f32[256,256]{1,0:T(8,128)S(1)}, u32[]{:S(2)}, u32[]{:S(2)}) collective-permute-start(f32[256,256]{1,0:T(8,128)S(1)} %collective-permute-done.1.refs_0_), channel_id=1, source_target_pairs={{0,3},{1,0},{2,1},{3,2},{4,7},{5,4},{6,5},{7,6},{8,11},{9,8},{10,9... | collective-permute-start | bytes 786440 | tf_op jit(solution)/shard_map/ppermute | solution.py:226
  60.8 0.0 collective-permute-start.3
  60.8 0.0 collective-permute-done.7.refs_3_
  60.8 0.0 collective-permute-done.6.refs_2_
  60.8 2.4 %products_near.1.refs_1_ = f32[4,256,256]{2,1,0:T(8,128)S(1)} custom-call(bf16[1024,256]{1,0:T(8,128)(2,1)S(1)} %labels.1.pi_ref, f32[256,256]{1,0:T(8,128)S(1)} %collective-permute-done.1.refs_0_, f32[256,256]{1,0:T(8,128)S(1)} %collective-permute-done.2.refs_1_, f32[256,256]{1,0:T(8,128)S(1)} %collective-permute-done.6.refs_2_, ...), custom_call_target="tpu_custom_call" | custom-call | flops 2147483648 | bytes 3145728 | tf_op jit(solution)/shard_map/products_near/pallas_call | solution.py:198
  63.2 0.8 %products_far.1.refs_2_ = f32[4,256,256]{2,1,0:T(8,128)S(1)} custom-call(bf16[1024,256]{1,0:T(8,128)(2,1)S(1)} %labels.1.pi_ref, f32[256,256]{1,0:T(8,128)S(1)} %collective-permute-done.5.refs_0_, f32[4,256,256]{2,1,0:T(8,128)S(1)} %products_near.1.refs_1_), custom_call_target="tpu_custom_call" | custom-call | flops 536870912 | bytes 2359296 | tf_op jit(solution)/shard_map/products_far/pallas_call | solution.py:198
  63.9 0.7 %collective-permute-done.4.refs_1_ = f32[256,256]{1,0:T(8,128)S(1)} collective-permute-done((f32[256,256]{1,0:T(8,128)S(1)}, f32[256,256]{1,0:T(8,128)S(1)}, u32[]{:S(2)}, u32[]{:S(2)}) %collective-permute-start.4) | collective-permute-done | bytes 262176 | tf_op jit(solution)/shard_map/ppermute | solution.py:226
  64.7 3.7 %collective-permute-done.3.refs_0_ = f32[256,256]{1,0:T(8,128)S(1)} collective-permute-done((f32[256,256]{1,0:T(8,128)S(1)}, f32[256,256]{1,0:T(8,128)S(1)}, u32[]{:S(2)}, u32[]{:S(2)}) %collective-permute-start.3) | collective-permute-done | bytes 262176 | tf_op jit(solution)/shard_map/ppermute | solution.py:225
  68.3 2.0 %products_last.1 = f32[4,256,256]{2,1,0:T(8,128)} custom-call(bf16[1024,256]{1,0:T(8,128)(2,1)S(1)} %labels.1.pi_ref, f32[256,256]{1,0:T(8,128)S(1)} %collective-permute-done.3.refs_0_, f32[256,256]{1,0:T(8,128)S(1)} %collective-permute-done.4.refs_1_, f32[4,256,256]{2,1,0:T(8,128)S(1)} %products_far.1.refs_2_), custom_call_target="tpu_custom_call" | custom-call | flops 1073741824 | bytes 2621440 | tf_op jit(solution)/shard_map/products_last/pallas_call | solution.py:198
  (13 shorter events, 0.0 us)
Async XLA Ops:
  0.0 28.7 %copy-start.2 = (s32[1,32]{1,0:T(1,128)S(1)}, s32[1,32]{1,0:T(1,128)}, u32[]{:S(2)}) copy-start(s32[1,32]{1,0:T(1,128)} %targets_ref.1) | copy-start | bytes 388
  0.0 52.2 %copy-start.1 = (s32[16,16]{1,0:T(8,128)S(1)}, s32[16,16]{1,0:T(8,128)}, u32[]{:S(2)}) copy-start(s32[16,16]{1,0:T(8,128)} %ms_ref.1) | copy-start | bytes 3076
  0.0 52.2 %copy-start.3 = (s32[4]{0:T(128)S(1)}, s32[4]{0:T(128)}, u32[]{:S(2)}) copy-start(s32[4]{0:T(128)} %own_ref.1) | copy-start | bytes 52
  0.0 52.2 %copy-start.4 = (s32[32]{0:T(128)S(1)}, s32[32]{0:T(128)}, u32[]{:S(2)}) copy-start(s32[32]{0:T(128)} %tm_ref.1) | copy-start | bytes 388
  0.0 52.2 %copy-start.5 = (s32[32]{0:T(128)S(1)}, s32[32]{0:T(128)}, u32[]{:S(2)}) copy-start(s32[32]{0:T(128)} %tf_ref.1) | copy-start | bytes 388
  0.0 53.0 %copy-start = (f32[1,4,256,256]{3,2,1,0:T(8,128)S(1)}, f32[1,4,256,256]{3,2,1,0:T(8,128)}, u32[]{:S(2)}) copy-start(f32[1,4,256,256]{3,2,1,0:T(8,128)} %param.21) | copy-start | bytes 3145732
  27.1 1.5 %collective-permute-start = (f32[16,16,256]{2,1,0:T(8,128)S(1)}, f32[16,16,256]{2,1,0:T(8,128)S(1)}, u32[]{:S(2)}, u32[]{:S(2)}) collective-permute-start(f32[16,16,256]{2,1,0:T(8,128)S(1)} %all_to_all.10.own_ref), channel_id=1, source_target_pairs={{0,8},{8,0},{16,24},{24,16},{32,40},{40,32},{48,56},{56,48},{64,72... | collective-permute-start | bytes 786440 | tf_op jit(solution)/shard_map/ppermute | solution.py:139
  44.2 9.6 %collective-permute-start.2 = (f32[256,256]{1,0:T(8,128)S(1)}, f32[256,256]{1,0:T(8,128)S(1)}, u32[]{:S(2)}, u32[]{:S(2)}) collective-permute-start(f32[256,256]{1,0:T(8,128)S(1)} %bitcast.10), channel_id=1, source_target_pairs={{0,2},{1,3},{2,0},{3,1},{4,6},{5,7},{6,4},{7,5},{8,10},{9,11},{10,... | collective-permute-start | bytes 786440 | tf_op jit(solution)/shard_map/ppermute | solution.py:217
  47.4 10.3 %collective-permute-start.1 = (f32[256,256]{1,0:T(8,128)S(1)}, f32[256,256]{1,0:T(8,128)S(1)}, u32[]{:S(2)}, u32[]{:S(2)}) collective-permute-start(f32[256,256]{1,0:T(8,128)S(1)} %bitcast.11), channel_id=1, source_target_pairs={{0,4},{1,5},{2,6},{3,7},{4,0},{5,1},{6,2},{7,3},{8,12},{9,13},{10,... | collective-permute-start | bytes 786440 | tf_op jit(solution)/shard_map/ppermute | solution.py:218
  50.1 10.6 %collective-permute-start.7 = (f32[256,256]{1,0:T(8,128)S(1)}, f32[256,256]{1,0:T(8,128)S(1)}, u32[]{:S(2)}, u32[]{:S(2)}) collective-permute-start(f32[256,256]{1,0:T(8,128)S(1)} %bitcast.12), channel_id=1, source_target_pairs={{0,3},{1,0},{2,1},{3,2},{4,7},{5,4},{6,5},{7,6},{8,11},{9,8},{10,9... | collective-permute-start | bytes 786440 | tf_op jit(solution)/shard_map/ppermute | solution.py:220
  51.2 9.6 %collective-permute-start.6 = (f32[256,256]{1,0:T(8,128)S(1)}, f32[256,256]{1,0:T(8,128)S(1)}, u32[]{:S(2)}, u32[]{:S(2)}) collective-permute-start(f32[256,256]{1,0:T(8,128)S(1)} %bitcast.13), channel_id=1, source_target_pairs={{0,1},{1,2},{2,3},{3,0},{4,5},{5,6},{6,7},{7,4},{8,9},{9,10},{10,1... | collective-permute-start | bytes 786440 | tf_op jit(solution)/shard_map/ppermute | solution.py:219
  53.8 9.4 %collective-permute-start.5 = (f32[256,256]{1,0:T(8,128)S(1)}, f32[256,256]{1,0:T(8,128)S(1)}, u32[]{:S(2)}, u32[]{:S(2)}) collective-permute-start(f32[256,256]{1,0:T(8,128)S(1)} %collective-permute-done.2.refs_1_), channel_id=1, source_target_pairs={{0,4},{1,5},{2,6},{3,7},{4,0},{5,1},{6,2},{7,3},{8,12},{9,13},{10,... | collective-permute-start | bytes 786440 | tf_op jit(solution)/shard_map/ppermute | solution.py:223
  57.7 6.9 %collective-permute-start.4 = (f32[256,256]{1,0:T(8,128)S(1)}, f32[256,256]{1,0:T(8,128)S(1)}, u32[]{:S(2)}, u32[]{:S(2)}) collective-permute-start(f32[256,256]{1,0:T(8,128)S(1)} %collective-permute-done.1.refs_0_), channel_id=1, source_target_pairs={{0,3},{1,0},{2,1},{3,2},{4,7},{5,4},{6,5},{7,6},{8,11},{9,8},{10,9... | collective-permute-start | bytes 786440 | tf_op jit(solution)/shard_map/ppermute | solution.py:226
  60.8 7.6 %collective-permute-start.3 = (f32[256,256]{1,0:T(8,128)S(1)}, f32[256,256]{1,0:T(8,128)S(1)}, u32[]{:S(2)}, u32[]{:S(2)}) collective-permute-start(f32[256,256]{1,0:T(8,128)S(1)} %collective-permute-done.1.refs_0_), channel_id=1, source_target_pairs={{0,1},{1,2},{2,3},{3,0},{4,5},{5,6},{6,7},{7,4},{8,9},{9,10},{10,1... | collective-permute-start | bytes 786440 | tf_op jit(solution)/shard_map/ppermute | solution.py:225

commit v6 on v5

--- a/solution.py
+++ b/solution.py
@@ -226,7 +226,8 @@
     beside_above = lax.ppermute(beside, "blk", downward)
     total = products(scale, pi, [beside, far, below, above], total, "products_near")
     total = products(scale, pi, [beside_far], total, "products_far")
-    return products(scale, pi, [beside_below, beside_above], total, "products_last", last=True)
+    total = products(scale, pi, [beside_above], total, "products_above")
+    return products(scale, pi, [beside_below], total, "products_last", last=True)
 
 
 def shards(

time: 70.7 us -> 70.3 us (level)
  waiting for transfers between devices: 5.95 us -> 5.19 us
    ppermute x1, waiting for transfers between devices: 3.69 us -> 2.94 us  [cycle_products(): beside_below = lax.ppermute(beside, 'blk', upward)]
    pallas_call x4 -> x5, Pallas kernels: 5.93 us -> 6.27 us  [products(): pl.pallas_call(functools.partial(products_kernel, scale, last), out_shape...]
  transfers between devices with their start and end apart: 8 -> 8, of which waited for: 3 -> 3; matrix products, arithmetic and copies ran while one was open for 0% -> 0% of each run, Pallas kernels for 7% -> 8%
where the time goes in v6:
time: 70.3 us; the launch traced here: 70.1 us
  blocking collectives  34.1 us (49%)
  Pallas kernels  15.6 us (22%)
  starting transfers between devices  14.9 us (21%)
  waiting for transfers between devices  5.19 us (7%)
    all_to_all x1, blocking collectives, permute_walkers(): lax.all_to_all(chunks, 'grp', 0, 0, axis_index_groups=alike, tiled=True)  19.4 us
    all_to_all x1, blocking collectives, permute_walkers(): lax.all_to_all(routed, 'grp', 0, 0, axis_index_groups=alike, tiled=True)  14.7 us
    pallas_call x1, Pallas kernels, walker(): pl.pallas_call(walker_kernel, out_shape=jax.ShapeDtypeStruct((KW, KW), F3...  7.71 us
    pallas_call x5, Pallas kernels, products(): pl.pallas_call(functools.partial(products_kernel, scale, last), out_shape...  6.27 us
    ppermute x1, starting transfers between devices, cycle_products(): beside_far = lax.ppermute(far, 'blk', across)  3.91 us
    ppermute x1, starting transfers between devices, cycle_products(): far = lax.ppermute(own, 'blk', opposite)  3.19 us
    ppermute x1, starting transfers between devices, cycle_products(): beside_above = lax.ppermute(beside, 'blk', downward)  3.06 us
    ppermute x1, waiting for transfers between devices, cycle_products(): beside_below = lax.ppermute(beside, 'blk', upward)  2.94 us
  transfers between devices with their start and end apart: 8, of which 3 were waited for; matrix products, arithmetic and copies ran while one was open for 0% of the time, Pallas kernels for 8%

profile of v6, /device:TPU:32, one launch (start us, length us, event | category | flops | bytes accessed | tf_op | source)
XLA Modules:
  0.0 70.1 jit_solution(15142640184170399340)
XLA Ops:
  0.0 7.7 %walker.1 = f32[256,256]{1,0:T(8,128)S(1)} custom-call(f32[1024,1024]{1,0:T(8,128)} %bitcast.15, bf16[4,1024,256]{2,1,0:T(8,128)(2,1)} %bitcast.16, s32[4,256]{1,0:T(4,128)} %bitcast.17, f32[1024,256]{1,0:T(8,128)} %l_hbm.1, f32[1024,256]{1,0:T(8,128)} %r_hbm.1), custom_call_target="tpu_custom_call" | custom-call | tf_op jit(solution)/shard_map/walker/pallas_call | solution.py:90
  7.8 19.4 %all_to_all.10.own_ref = f32[16,16,256]{2,1,0:T(8,128)S(1)} all-to-all(f32[16,16,256]{2,1,0:T(8,128)S(1)} %bitcast.8), channel_id=1, replica_groups={{0,16,32,48,64,80,96,112,128,144,160,176,192,208,224,240},{8,24,40,56,7..., dimensions={0} | all-to-all | bytes 524288 | tf_op jit(solution)/shard_map/all_to_all | solution.py:138
  27.1 0.0 collective-permute-start
  27.1 1.5 %collective-permute-done.other_ref = f32[16,16,256]{2,1,0:T(8,128)S(1)} collective-permute-done((f32[16,16,256]{2,1,0:T(8,128)S(1)}, f32[16,16,256]{2,1,0:T(8,128)S(1)}, u32[]{:S(2)}, u32[]{:S(2)}) %collective-permute-start) | collective-permute-done | bytes 262176 | tf_op jit(solution)/shard_map/ppermute | solution.py:139
  28.7 0.8 %route.1 = f32[16,16,256]{2,1,0:T(8,128)S(1)} custom-call(s32[1]{0:T(128)} %bitcast.core_ref, s32[1,32]{1,0:T(1,128)S(1)} %copy-done.2, f32[16,16,256]{2,1,0:T(8,128)S(1)} %all_to_all.10.own_ref, f32[16,16,256]{2,1,0:T(8,128)S(1)} %collective-permute-done.other_ref), custom_call_target="tpu_custom_call" | custom-call | tf_op jit(solution)/shard_map/route/pallas_call | solution.py:122
  29.5 14.7 %all_to_all.11 = f32[16,16,256]{2,1,0:T(8,128)S(1)} all-to-all(f32[16,16,256]{2,1,0:T(8,128)S(1)} %route.1), channel_id=1, replica_groups={{0,16,32,48,64,80,96,112,128,144,160,176,192,208,224,240},{8,24,40,56,7..., dimensions={0} | all-to-all | bytes 524288 | tf_op jit(solution)/shard_map/all_to_all | solution.py:141
  44.2 3.2 %collective-permute-start.2 = (f32[256,256]{1,0:T(8,128)S(1)}, f32[256,256]{1,0:T(8,128)S(1)}, u32[]{:S(2)}, u32[]{:S(2)}) collective-permute-start(f32[256,256]{1,0:T(8,128)S(1)} %bitcast.10), channel_id=1, source_target_pairs={{0,2},{1,3},{2,0},{3,1},{4,6},{5,7},{6,4},{7,5},{8,10},{9,11},{10,... | collective-permute-start | bytes 786440 | tf_op jit(solution)/shard_map/ppermute | solution.py:217
  47.4 2.7 %collective-permute-start.1 = (f32[256,256]{1,0:T(8,128)S(1)}, f32[256,256]{1,0:T(8,128)S(1)}, u32[]{:S(2)}, u32[]{:S(2)}) collective-permute-start(f32[256,256]{1,0:T(8,128)S(1)} %bitcast.11), channel_id=1, source_target_pairs={{0,4},{1,5},{2,6},{3,7},{4,0},{5,1},{6,2},{7,3},{8,12},{9,13},{10,... | collective-permute-start | bytes 786440 | tf_op jit(solution)/shard_map/ppermute | solution.py:218
  50.1 1.1 %collective-permute-start.7 = (f32[256,256]{1,0:T(8,128)S(1)}, f32[256,256]{1,0:T(8,128)S(1)}, u32[]{:S(2)}, u32[]{:S(2)}) collective-permute-start(f32[256,256]{1,0:T(8,128)S(1)} %bitcast.12), channel_id=1, source_target_pairs={{0,3},{1,0},{2,1},{3,2},{4,7},{5,4},{6,5},{7,6},{8,11},{9,8},{10,9... | collective-permute-start | bytes 786440 | tf_op jit(solution)/shard_map/ppermute | solution.py:220
  51.2 1.0 %collective-permute-start.6 = (f32[256,256]{1,0:T(8,128)S(1)}, f32[256,256]{1,0:T(8,128)S(1)}, u32[]{:S(2)}, u32[]{:S(2)}) collective-permute-start(f32[256,256]{1,0:T(8,128)S(1)} %bitcast.13), channel_id=1, source_target_pairs={{0,1},{1,2},{2,3},{3,0},{4,5},{5,6},{6,7},{7,4},{8,9},{9,10},{10,1... | collective-permute-start | bytes 786440 | tf_op jit(solution)/shard_map/ppermute | solution.py:219
  52.2 0.8 %labels.1.pi_ref = bf16[1024,256]{1,0:T(8,128)(2,1)S(1)} custom-call(s32[4]{0:T(128)S(1)} %copy-done.3, s32[16,16]{1,0:T(8,128)S(1)} %copy-done.1, s32[32]{0:T(128)S(1)} %copy-done.4, s32[32]{0:T(128)S(1)} %copy-done.5), custom_call_target="tpu_custom_call" | custom-call | flops 4000000 | bytes 1000000 | tf_op jit(solution)/shard_map/labels/pallas_call | solution.py:158
  53.0 0.7 %products_own.1.refs_4_ = f32[4,256,256]{2,1,0:T(8,128)S(1)} custom-call(bf16[1024,256]{1,0:T(8,128)(2,1)S(1)} %labels.1.pi_ref, f32[256,256]{1,0:T(8,128)S(1)} %bitcast.14, f32[4,256,256]{2,1,0:T(8,128)S(1)} %bitcast.9), custom_call_target="tpu_custom_call" | custom-call | flops 536870912 | bytes 2359296 | tf_op jit(solution)/shard_map/products_own/pallas_call | solution.py:198
  53.8 3.9 %collective-permute-start.5 = (f32[256,256]{1,0:T(8,128)S(1)}, f32[256,256]{1,0:T(8,128)S(1)}, u32[]{:S(2)}, u32[]{:S(2)}) collective-permute-start(f32[256,256]{1,0:T(8,128)S(1)} %collective-permute-done.2.refs_1_), channel_id=1, source_target_pairs={{0,4},{1,5},{2,6},{3,7},{4,0},{5,1},{6,2},{7,3},{8,12},{9,13},{10,... | collective-permute-start | bytes 786440 | tf_op jit(solution)/shard_map/ppermute | solution.py:223
  57.7 0.0 collective-permute-done.1.refs_0_
  57.7 3.1 %collective-permute-start.4 = (f32[256,256]{1,0:T(8,128)S(1)}, f32[256,256]{1,0:T(8,128)S(1)}, u32[]{:S(2)}, u32[]{:S(2)}) collective-permute-start(f32[256,256]{1,0:T(8,128)S(1)} %collective-permute-done.1.refs_0_), channel_id=1, source_target_pairs={{0,3},{1,0},{2,1},{3,2},{4,7},{5,4},{6,5},{7,6},{8,11},{9,8},{10,9... | collective-permute-start | bytes 786440 | tf_op jit(solution)/shard_map/ppermute | solution.py:226
  60.8 0.0 collective-permute-start.3
  60.8 0.0 collective-permute-done.7.refs_3_
  60.8 0.0 collective-permute-done.6.refs_2_
  60.8 2.4 %products_near.1.refs_1_ = f32[4,256,256]{2,1,0:T(8,128)S(1)} custom-call(bf16[1024,256]{1,0:T(8,128)(2,1)S(1)} %labels.1.pi_ref, f32[256,256]{1,0:T(8,128)S(1)} %collective-permute-done.1.refs_0_, f32[256,256]{1,0:T(8,128)S(1)} %collective-permute-done.2.refs_1_, f32[256,256]{1,0:T(8,128)S(1)} %collective-permute-done.6.refs_2_, ...), custom_call_target="tpu_custom_call" | custom-call | flops 2147483648 | bytes 3145728 | tf_op jit(solution)/shard_map/products_near/pallas_call | solution.py:198
  63.2 0.8 %products_far.1.refs_1_ = f32[4,256,256]{2,1,0:T(8,128)S(1)} custom-call(bf16[1024,256]{1,0:T(8,128)(2,1)S(1)} %labels.1.pi_ref, f32[256,256]{1,0:T(8,128)S(1)} %collective-permute-done.5.refs_0_, f32[4,256,256]{2,1,0:T(8,128)S(1)} %products_near.1.refs_1_), custom_call_target="tpu_custom_call" | custom-call | flops 536870912 | bytes 2359296 | tf_op jit(solution)/shard_map/products_far/pallas_call | solution.py:198
  63.9 0.7 %collective-permute-done.4.refs_0_ = f32[256,256]{1,0:T(8,128)S(1)} collective-permute-done((f32[256,256]{1,0:T(8,128)S(1)}, f32[256,256]{1,0:T(8,128)S(1)}, u32[]{:S(2)}, u32[]{:S(2)}) %collective-permute-start.4) | collective-permute-done | bytes 262176 | tf_op jit(solution)/shard_map/ppermute | solution.py:226
  64.7 0.7 %products_above.1.refs_1_ = f32[4,256,256]{2,1,0:T(8,128)S(1)} custom-call(bf16[1024,256]{1,0:T(8,128)(2,1)S(1)} %labels.1.pi_ref, f32[256,256]{1,0:T(8,128)S(1)} %collective-permute-done.4.refs_0_, f32[4,256,256]{2,1,0:T(8,128)S(1)} %products_far.1.refs_1_), custom_call_target="tpu_custom_call" | custom-call | flops 536870912 | bytes 2359296 | tf_op jit(solution)/shard_map/products_above/pallas_call | solution.py:198
  65.4 2.9 %collective-permute-done.3.refs_0_ = f32[256,256]{1,0:T(8,128)S(1)} collective-permute-done((f32[256,256]{1,0:T(8,128)S(1)}, f32[256,256]{1,0:T(8,128)S(1)}, u32[]{:S(2)}, u32[]{:S(2)}) %collective-permute-start.3) | collective-permute-done | bytes 262176 | tf_op jit(solution)/shard_map/ppermute | solution.py:225
  68.3 1.6 %products_last.1 = f32[4,256,256]{2,1,0:T(8,128)} custom-call(bf16[1024,256]{1,0:T(8,128)(2,1)S(1)} %labels.1.pi_ref, f32[256,256]{1,0:T(8,128)S(1)} %collective-permute-done.3.refs_0_, f32[4,256,256]{2,1,0:T(8,128)S(1)} %products_above.1.refs_1_), custom_call_target="tpu_custom_call" | custom-call | flops 536870912 | bytes 2359296 | tf_op jit(solution)/shard_map/products_last/pallas_call | solution.py:198
  (14 shorter events, 0.0 us)
Async XLA Ops:
  0.0 28.7 %copy-start.2 = (s32[1,32]{1,0:T(1,128)S(1)}, s32[1,32]{1,0:T(1,128)}, u32[]{:S(2)}) copy-start(s32[1,32]{1,0:T(1,128)} %targets_ref.1) | copy-start | bytes 388
  0.0 52.2 %copy-start.1 = (s32[16,16]{1,0:T(8,128)S(1)}, s32[16,16]{1,0:T(8,128)}, u32[]{:S(2)}) copy-start(s32[16,16]{1,0:T(8,128)} %ms_ref.1) | copy-start | bytes 3076
  0.0 52.2 %copy-start.3 = (s32[4]{0:T(128)S(1)}, s32[4]{0:T(128)}, u32[]{:S(2)}) copy-start(s32[4]{0:T(128)} %own_ref.1) | copy-start | bytes 52
  0.0 52.2 %copy-start.4 = (s32[32]{0:T(128)S(1)}, s32[32]{0:T(128)}, u32[]{:S(2)}) copy-start(s32[32]{0:T(128)} %tm_ref.1) | copy-start | bytes 388
  0.0 52.2 %copy-start.5 = (s32[32]{0:T(128)S(1)}, s32[32]{0:T(128)}, u32[]{:S(2)}) copy-start(s32[32]{0:T(128)} %tf_ref.1) | copy-start | bytes 388
  0.0 53.0 %copy-start = (f32[1,4,256,256]{3,2,1,0:T(8,128)S(1)}, f32[1,4,256,256]{3,2,1,0:T(8,128)}, u32[]{:S(2)}) copy-start(f32[1,4,256,256]{3,2,1,0:T(8,128)} %param.21) | copy-start | bytes 3145732
  27.1 1.5 %collective-permute-start = (f32[16,16,256]{2,1,0:T(8,128)S(1)}, f32[16,16,256]{2,1,0:T(8,128)S(1)}, u32[]{:S(2)}, u32[]{:S(2)}) collective-permute-start(f32[16,16,256]{2,1,0:T(8,128)S(1)} %all_to_all.10.own_ref), channel_id=1, source_target_pairs={{0,8},{8,0},{16,24},{24,16},{32,40},{40,32},{48,56},{56,48},{64,72... | collective-permute-start | bytes 786440 | tf_op jit(solution)/shard_map/ppermute | solution.py:139
  44.2 9.6 %collective-permute-start.2 = (f32[256,256]{1,0:T(8,128)S(1)}, f32[256,256]{1,0:T(8,128)S(1)}, u32[]{:S(2)}, u32[]{:S(2)}) collective-permute-start(f32[256,256]{1,0:T(8,128)S(1)} %bitcast.10), channel_id=1, source_target_pairs={{0,2},{1,3},{2,0},{3,1},{4,6},{5,7},{6,4},{7,5},{8,10},{9,11},{10,... | collective-permute-start | bytes 786440 | tf_op jit(solution)/shard_map/ppermute | solution.py:217
  47.4 10.3 %collective-permute-start.1 = (f32[256,256]{1,0:T(8,128)S(1)}, f32[256,256]{1,0:T(8,128)S(1)}, u32[]{:S(2)}, u32[]{:S(2)}) collective-permute-start(f32[256,256]{1,0:T(8,128)S(1)} %bitcast.11), channel_id=1, source_target_pairs={{0,4},{1,5},{2,6},{3,7},{4,0},{5,1},{6,2},{7,3},{8,12},{9,13},{10,... | collective-permute-start | bytes 786440 | tf_op jit(solution)/shard_map/ppermute | solution.py:218
  50.1 10.6 %collective-permute-start.7 = (f32[256,256]{1,0:T(8,128)S(1)}, f32[256,256]{1,0:T(8,128)S(1)}, u32[]{:S(2)}, u32[]{:S(2)}) collective-permute-start(f32[256,256]{1,0:T(8,128)S(1)} %bitcast.12), channel_id=1, source_target_pairs={{0,3},{1,0},{2,1},{3,2},{4,7},{5,4},{6,5},{7,6},{8,11},{9,8},{10,9... | collective-permute-start | bytes 786440 | tf_op jit(solution)/shard_map/ppermute | solution.py:220
  51.2 9.6 %collective-permute-start.6 = (f32[256,256]{1,0:T(8,128)S(1)}, f32[256,256]{1,0:T(8,128)S(1)}, u32[]{:S(2)}, u32[]{:S(2)}) collective-permute-start(f32[256,256]{1,0:T(8,128)S(1)} %bitcast.13), channel_id=1, source_target_pairs={{0,1},{1,2},{2,3},{3,0},{4,5},{5,6},{6,7},{7,4},{8,9},{9,10},{10,1... | collective-permute-start | bytes 786440 | tf_op jit(solution)/shard_map/ppermute | solution.py:219
  53.8 9.4 %collective-permute-start.5 = (f32[256,256]{1,0:T(8,128)S(1)}, f32[256,256]{1,0:T(8,128)S(1)}, u32[]{:S(2)}, u32[]{:S(2)}) collective-permute-start(f32[256,256]{1,0:T(8,128)S(1)} %collective-permute-done.2.refs_1_), channel_id=1, source_target_pairs={{0,4},{1,5},{2,6},{3,7},{4,0},{5,1},{6,2},{7,3},{8,12},{9,13},{10,... | collective-permute-start | bytes 786440 | tf_op jit(solution)/shard_map/ppermute | solution.py:223
  57.7 6.9 %collective-permute-start.4 = (f32[256,256]{1,0:T(8,128)S(1)}, f32[256,256]{1,0:T(8,128)S(1)}, u32[]{:S(2)}, u32[]{:S(2)}) collective-permute-start(f32[256,256]{1,0:T(8,128)S(1)} %collective-permute-done.1.refs_0_), channel_id=1, source_target_pairs={{0,3},{1,0},{2,1},{3,2},{4,7},{5,4},{6,5},{7,6},{8,11},{9,8},{10,9... | collective-permute-start | bytes 786440 | tf_op jit(solution)/shard_map/ppermute | solution.py:226
  60.8 7.6 %collective-permute-start.3 = (f32[256,256]{1,0:T(8,128)S(1)}, f32[256,256]{1,0:T(8,128)S(1)}, u32[]{:S(2)}, u32[]{:S(2)}) collective-permute-start(f32[256,256]{1,0:T(8,128)S(1)} %collective-permute-done.1.refs_0_), channel_id=1, source_target_pairs={{0,1},{1,2},{2,3},{3,0},{4,5},{5,6},{6,7},{7,4},{8,9},{9,10},{10,1... | collective-permute-start | bytes 786440 | tf_op jit(solution)/shard_map/ppermute | solution.py:225

commit v7 on v6

--- a/solution.py
+++ b/solution.py
@@ -129,7 +129,7 @@
     )(core, targets, own, other)
 
 
-def permute_walkers(greens, targets):
+def permute_walkers(greens, targets, pi):
     n_grp = lax.axis_size("grp")
     pairs = n_grp // 2
     core = lax.axis_index("grp") & 1
@@ -137,8 +137,9 @@
     chunks = greens.reshape(pairs, KW // pairs, KW)
     own = lax.all_to_all(chunks, "grp", 0, 0, axis_index_groups=alike, tiled=True)
     other = lax.ppermute(own, "grp", [(w, w ^ 1) for w in range(n_grp)])
+    other, pi = lax.optimization_barrier((other, pi))
     routed = route(core.reshape(1), targets, own, other)
-    return lax.all_to_all(routed, "grp", 0, 0, axis_index_groups=alike, tiled=True).reshape(KW, KW)
+    return lax.all_to_all(routed, "grp", 0, 0, axis_index_groups=alike, tiled=True).reshape(KW, KW), pi
 
 
 def labels_kernel(own_ref, ms_ref, tm_ref, tf_ref, pi_ref):
@@ -236,7 +237,7 @@
 ):
     pi = labels(ownership, momentum_sum, transfer_momentum, transfer_frequency)
     greens = walker(walker_matrix[0, 0], updates[0, 0], update_rows[0, 0], left_table, right_table)
-    measured = permute_walkers(greens, assignment)
+    measured, pi = permute_walkers(greens, assignment, pi)
     scale = 1.0 / lax.axis_size("blk")
     return cycle_products(scale, pi, measured, g4_prior[0])[None]
 

time: 70.3 us -> 70.3 us (level)
    ppermute x1, waiting for transfers between devices: 1.53 us -> 0.67 us  [permute_walkers(): other = lax.ppermute(own, 'grp', [(w, w ^ 1) for w in range(n_grp)])]
  transfers between devices with their start and end apart: 8 -> 8, of which waited for: 3 -> 4; matrix products, arithmetic and copies ran while one was open for 0% -> 0% of each run, Pallas kernels for 8% -> 8%
where the time goes in v7:
time: 70.3 us; the launch traced here: 70.1 us
  blocking collectives  34.1 us (49%)
  Pallas kernels  15.6 us (22%)
  starting transfers between devices  15.1 us (21%)
  waiting for transfers between devices  5.03 us (7%)
    all_to_all x1, blocking collectives, permute_walkers(): lax.all_to_all(chunks, 'grp', 0, 0, axis_index_groups=alike, tiled=True)  19.4 us
    all_to_all x1, blocking collectives, permute_walkers(): lax.all_to_all(routed, 'grp', 0, 0, axis_index_groups=alike, tiled=True)  14.7 us
    pallas_call x1, Pallas kernels, walker(): pl.pallas_call(walker_kernel, out_shape=jax.ShapeDtypeStruct((KW, KW), F3...  7.71 us
    pallas_call x5, Pallas kernels, products(): pl.pallas_call(functools.partial(products_kernel, scale, last), out_shape...  6.27 us
    ppermute x1, starting transfers between devices, cycle_products(): beside_far = lax.ppermute(far, 'blk', across)  4.08 us
    ppermute x1, starting transfers between devices, cycle_products(): far = lax.ppermute(own, 'blk', opposite)  3.19 us
    ppermute x1, starting transfers between devices, cycle_products(): beside_above = lax.ppermute(beside, 'blk', downward)  3.06 us
    ppermute x1, waiting for transfers between devices, cycle_products(): beside_below = lax.ppermute(beside, 'blk', upward)  2.94 us
  transfers between devices with their start and end apart: 8, of which 4 were waited for; matrix products, arithmetic and copies ran while one was open for 0% of the time, Pallas kernels for 8%

profile of v7, /device:TPU:32, one launch (start us, length us, event | category | flops | bytes accessed | tf_op | source)
XLA Modules:
  0.0 70.1 jit_solution(17460641660726011198)
XLA Ops:
  0.0 7.7 %walker.1 = f32[256,256]{1,0:T(8,128)S(1)} custom-call(f32[1024,1024]{1,0:T(8,128)} %bitcast.15, bf16[4,1024,256]{2,1,0:T(8,128)(2,1)} %bitcast.16, s32[4,256]{1,0:T(4,128)} %bitcast.17, f32[1024,256]{1,0:T(8,128)} %l_hbm.1, f32[1024,256]{1,0:T(8,128)} %r_hbm.1), custom_call_target="tpu_custom_call" | custom-call | tf_op jit(solution)/shard_map/walker/pallas_call | solution.py:90
  7.8 19.4 %all_to_all.10.own_ref = f32[16,16,256]{2,1,0:T(8,128)S(1)} all-to-all(f32[16,16,256]{2,1,0:T(8,128)S(1)} %bitcast.8), channel_id=1, replica_groups={{0,16,32,48,64,80,96,112,128,144,160,176,192,208,224,240},{8,24,40,56,7..., dimensions={0} | all-to-all | bytes 524288 | tf_op jit(solution)/shard_map/all_to_all | solution.py:138
  27.1 0.0 collective-permute-start
  27.1 0.8 %labels.1.pi_ref = bf16[1024,256]{1,0:T(8,128)(2,1)S(1)} custom-call(s32[4]{0:T(128)S(1)} %copy-done.2, s32[16,16]{1,0:T(8,128)S(1)} %copy-done.1, s32[32]{0:T(128)S(1)} %copy-done.3, s32[32]{0:T(128)S(1)} %copy-done.4), custom_call_target="tpu_custom_call" | custom-call | flops 4000000 | bytes 1000000 | tf_op jit(solution)/shard_map/labels/pallas_call | solution.py:159
  28.0 0.7 collective-permute-done.other_ref
  28.7 0.8 %route.1 = f32[16,16,256]{2,1,0:T(8,128)S(1)} custom-call(s32[1]{0:T(128)} %bitcast.4.core_ref, s32[1,32]{1,0:T(1,128)S(1)} %copy-done.5, f32[16,16,256]{2,1,0:T(8,128)S(1)} %all_to_all.10.own_ref, f32[16,16,256]{2,1,0:T(8,128)S(1)} %collective-permute-done.other_ref), custom_call_target="tpu_custom_call" | custom-call | tf_op jit(solution)/shard_map/route/pallas_call | solution.py:122
  29.5 14.7 %all_to_all.11 = f32[16,16,256]{2,1,0:T(8,128)S(1)} all-to-all(f32[16,16,256]{2,1,0:T(8,128)S(1)} %route.1), channel_id=1, replica_groups={{0,16,32,48,64,80,96,112,128,144,160,176,192,208,224,240},{8,24,40,56,7..., dimensions={0} | all-to-all | bytes 524288 | tf_op jit(solution)/shard_map/all_to_all | solution.py:142
  44.2 3.2 %collective-permute-start.2 = (f32[256,256]{1,0:T(8,128)S(1)}, f32[256,256]{1,0:T(8,128)S(1)}, u32[]{:S(2)}, u32[]{:S(2)}) collective-permute-start(f32[256,256]{1,0:T(8,128)S(1)} %bitcast.10), channel_id=1, source_target_pairs={{0,2},{1,3},{2,0},{3,1},{4,6},{5,7},{6,4},{7,5},{8,10},{9,11},{10,... | collective-permute-start | bytes 786440 | tf_op jit(solution)/shard_map/ppermute | solution.py:218
  47.4 2.7 %collective-permute-start.1 = (f32[256,256]{1,0:T(8,128)S(1)}, f32[256,256]{1,0:T(8,128)S(1)}, u32[]{:S(2)}, u32[]{:S(2)}) collective-permute-start(f32[256,256]{1,0:T(8,128)S(1)} %bitcast.11), channel_id=1, source_target_pairs={{0,4},{1,5},{2,6},{3,7},{4,0},{5,1},{6,2},{7,3},{8,12},{9,13},{10,... | collective-permute-start | bytes 786440 | tf_op jit(solution)/shard_map/ppermute | solution.py:219
  50.1 1.1 %collective-permute-start.7 = (f32[256,256]{1,0:T(8,128)S(1)}, f32[256,256]{1,0:T(8,128)S(1)}, u32[]{:S(2)}, u32[]{:S(2)}) collective-permute-start(f32[256,256]{1,0:T(8,128)S(1)} %bitcast.12), channel_id=1, source_target_pairs={{0,3},{1,0},{2,1},{3,2},{4,7},{5,4},{6,5},{7,6},{8,11},{9,8},{10,9... | collective-permute-start | bytes 786440 | tf_op jit(solution)/shard_map/ppermute | solution.py:221
  51.2 1.0 %collective-permute-start.6 = (f32[256,256]{1,0:T(8,128)S(1)}, f32[256,256]{1,0:T(8,128)S(1)}, u32[]{:S(2)}, u32[]{:S(2)}) collective-permute-start(f32[256,256]{1,0:T(8,128)S(1)} %bitcast.13), channel_id=1, source_target_pairs={{0,1},{1,2},{2,3},{3,0},{4,5},{5,6},{6,7},{7,4},{8,9},{9,10},{10,1... | collective-permute-start | bytes 786440 | tf_op jit(solution)/shard_map/ppermute | solution.py:220
  52.2 0.7 %products_own.1.refs_4_ = f32[4,256,256]{2,1,0:T(8,128)S(1)} custom-call(bf16[1024,256]{1,0:T(8,128)(2,1)S(1)} %labels.1.pi_ref, f32[256,256]{1,0:T(8,128)S(1)} %bitcast.14, f32[4,256,256]{2,1,0:T(8,128)S(1)} %bitcast.9), custom_call_target="tpu_custom_call" | custom-call | flops 536870912 | bytes 2359296 | tf_op jit(solution)/shard_map/products_own/pallas_call | solution.py:199
  52.9 0.7 collective-permute-done.2.refs_1_
  53.6 4.1 %collective-permute-start.5 = (f32[256,256]{1,0:T(8,128)S(1)}, f32[256,256]{1,0:T(8,128)S(1)}, u32[]{:S(2)}, u32[]{:S(2)}) collective-permute-start(f32[256,256]{1,0:T(8,128)S(1)} %collective-permute-done.2.refs_1_), channel_id=1, source_target_pairs={{0,4},{1,5},{2,6},{3,7},{4,0},{5,1},{6,2},{7,3},{8,12},{9,13},{10,... | collective-permute-start | bytes 786440 | tf_op jit(solution)/shard_map/ppermute | solution.py:224
  57.7 3.1 %collective-permute-start.4 = (f32[256,256]{1,0:T(8,128)S(1)}, f32[256,256]{1,0:T(8,128)S(1)}, u32[]{:S(2)}, u32[]{:S(2)}) collective-permute-start(f32[256,256]{1,0:T(8,128)S(1)} %collective-permute-done.1.refs_0_), channel_id=1, source_target_pairs={{0,3},{1,0},{2,1},{3,2},{4,7},{5,4},{6,5},{7,6},{8,11},{9,8},{10,9... | collective-permute-start | bytes 786440 | tf_op jit(solution)/shard_map/ppermute | solution.py:227
  60.8 0.0 collective-permute-start.3
  60.8 0.0 collective-permute-done.6.refs_2_
  60.8 2.4 %products_near.1.refs_1_ = f32[4,256,256]{2,1,0:T(8,128)S(1)} custom-call(bf16[1024,256]{1,0:T(8,128)(2,1)S(1)} %labels.1.pi_ref, f32[256,256]{1,0:T(8,128)S(1)} %collective-permute-done.1.refs_0_, f32[256,256]{1,0:T(8,128)S(1)} %collective-permute-done.2.refs_1_, f32[256,256]{1,0:T(8,128)S(1)} %collective-permute-done.6.refs_2_, ...), custom_call_target="tpu_custom_call" | custom-call | flops 2147483648 | bytes 3145728 | tf_op jit(solution)/shard_map/products_near/pallas_call | solution.py:199
  63.2 0.0 collective-permute-done.5.refs_0_
  63.2 0.7 %products_far.1.refs_1_ = f32[4,256,256]{2,1,0:T(8,128)S(1)} custom-call(bf16[1024,256]{1,0:T(8,128)(2,1)S(1)} %labels.1.pi_ref, f32[256,256]{1,0:T(8,128)S(1)} %collective-permute-done.5.refs_0_, f32[4,256,256]{2,1,0:T(8,128)S(1)} %products_near.1.refs_1_), custom_call_target="tpu_custom_call" | custom-call | flops 536870912 | bytes 2359296 | tf_op jit(solution)/shard_map/products_far/pallas_call | solution.py:199
  63.9 0.7 %collective-permute-done.4.refs_0_ = f32[256,256]{1,0:T(8,128)S(1)} collective-permute-done((f32[256,256]{1,0:T(8,128)S(1)}, f32[256,256]{1,0:T(8,128)S(1)}, u32[]{:S(2)}, u32[]{:S(2)}) %collective-permute-start.4) | collective-permute-done | bytes 262176 | tf_op jit(solution)/shard_map/ppermute | solution.py:227
  64.7 0.7 %products_above.1.refs_1_ = f32[4,256,256]{2,1,0:T(8,128)S(1)} custom-call(bf16[1024,256]{1,0:T(8,128)(2,1)S(1)} %labels.1.pi_ref, f32[256,256]{1,0:T(8,128)S(1)} %collective-permute-done.4.refs_0_, f32[4,256,256]{2,1,0:T(8,128)S(1)} %products_far.1.refs_1_), custom_call_target="tpu_custom_call" | custom-call | flops 536870912 | bytes 2359296 | tf_op jit(solution)/shard_map/products_above/pallas_call | solution.py:199
  65.4 2.9 %collective-permute-done.3.refs_0_ = f32[256,256]{1,0:T(8,128)S(1)} collective-permute-done((f32[256,256]{1,0:T(8,128)S(1)}, f32[256,256]{1,0:T(8,128)S(1)}, u32[]{:S(2)}, u32[]{:S(2)}) %collective-permute-start.3) | collective-permute-done | bytes 262176 | tf_op jit(solution)/shard_map/ppermute | solution.py:226
  68.3 1.6 %products_last.1 = f32[4,256,256]{2,1,0:T(8,128)} custom-call(bf16[1024,256]{1,0:T(8,128)(2,1)S(1)} %labels.1.pi_ref, f32[256,256]{1,0:T(8,128)S(1)} %collective-permute-done.3.refs_0_, f32[4,256,256]{2,1,0:T(8,128)S(1)} %products_above.1.refs_1_), custom_call_target="tpu_custom_call" | custom-call | flops 536870912 | bytes 2359296 | tf_op jit(solution)/shard_map/products_last/pallas_call | solution.py:199
  (14 shorter events, 0.0 us)
Async XLA Ops:
  0.0 27.1 %copy-start.1 = (s32[16,16]{1,0:T(8,128)S(1)}, s32[16,16]{1,0:T(8,128)}, u32[]{:S(2)}) copy-start(s32[16,16]{1,0:T(8,128)} %ms_ref.1) | copy-start | bytes 3076
  0.0 27.1 %copy-start.2 = (s32[4]{0:T(128)S(1)}, s32[4]{0:T(128)}, u32[]{:S(2)}) copy-start(s32[4]{0:T(128)} %own_ref.1) | copy-start | bytes 52
  0.0 27.1 %copy-start.3 = (s32[32]{0:T(128)S(1)}, s32[32]{0:T(128)}, u32[]{:S(2)}) copy-start(s32[32]{0:T(128)} %tm_ref.1) | copy-start | bytes 388
  0.0 27.1 %copy-start.4 = (s32[32]{0:T(128)S(1)}, s32[32]{0:T(128)}, u32[]{:S(2)}) copy-start(s32[32]{0:T(128)} %tf_ref.1) | copy-start | bytes 388
  0.0 28.6 %copy-start.5 = (s32[1,32]{1,0:T(1,128)S(1)}, s32[1,32]{1,0:T(1,128)}, u32[]{:S(2)}) copy-start(s32[1,32]{1,0:T(1,128)} %targets_ref.1) | copy-start | bytes 388
  0.0 52.1 %copy-start = (f32[1,4,256,256]{3,2,1,0:T(8,128)S(1)}, f32[1,4,256,256]{3,2,1,0:T(8,128)}, u32[]{:S(2)}) copy-start(f32[1,4,256,256]{3,2,1,0:T(8,128)} %param.21) | copy-start | bytes 3145732
  27.1 1.5 %collective-permute-start = (f32[16,16,256]{2,1,0:T(8,128)S(1)}, f32[16,16,256]{2,1,0:T(8,128)S(1)}, u32[]{:S(2)}, u32[]{:S(2)}) collective-permute-start(f32[16,16,256]{2,1,0:T(8,128)S(1)} %all_to_all.10.own_ref), channel_id=1, source_target_pairs={{0,8},{8,0},{16,24},{24,16},{32,40},{40,32},{48,56},{56,48},{64,72... | collective-permute-start | bytes 786440 | tf_op jit(solution)/shard_map/ppermute | solution.py:139
  44.2 9.4 %collective-permute-start.2 = (f32[256,256]{1,0:T(8,128)S(1)}, f32[256,256]{1,0:T(8,128)S(1)}, u32[]{:S(2)}, u32[]{:S(2)}) collective-permute-start(f32[256,256]{1,0:T(8,128)S(1)} %bitcast.10), channel_id=1, source_target_pairs={{0,2},{1,3},{2,0},{3,1},{4,6},{5,7},{6,4},{7,5},{8,10},{9,11},{10,... | collective-permute-start | bytes 786440 | tf_op jit(solution)/shard_map/ppermute | solution.py:218
  47.4 10.3 %collective-permute-start.1 = (f32[256,256]{1,0:T(8,128)S(1)}, f32[256,256]{1,0:T(8,128)S(1)}, u32[]{:S(2)}, u32[]{:S(2)}) collective-permute-start(f32[256,256]{1,0:T(8,128)S(1)} %bitcast.11), channel_id=1, source_target_pairs={{0,4},{1,5},{2,6},{3,7},{4,0},{5,1},{6,2},{7,3},{8,12},{9,13},{10,... | collective-permute-start | bytes 786440 | tf_op jit(solution)/shard_map/ppermute | solution.py:219
  50.1 10.6 %collective-permute-start.7 = (f32[256,256]{1,0:T(8,128)S(1)}, f32[256,256]{1,0:T(8,128)S(1)}, u32[]{:S(2)}, u32[]{:S(2)}) collective-permute-start(f32[256,256]{1,0:T(8,128)S(1)} %bitcast.12), channel_id=1, source_target_pairs={{0,3},{1,0},{2,1},{3,2},{4,7},{5,4},{6,5},{7,6},{8,11},{9,8},{10,9... | collective-permute-start | bytes 786440 | tf_op jit(solution)/shard_map/ppermute | solution.py:221
  51.2 9.6 %collective-permute-start.6 = (f32[256,256]{1,0:T(8,128)S(1)}, f32[256,256]{1,0:T(8,128)S(1)}, u32[]{:S(2)}, u32[]{:S(2)}) collective-permute-start(f32[256,256]{1,0:T(8,128)S(1)} %bitcast.13), channel_id=1, source_target_pairs={{0,1},{1,2},{2,3},{3,0},{4,5},{5,6},{6,7},{7,4},{8,9},{9,10},{10,1... | collective-permute-start | bytes 786440 | tf_op jit(solution)/shard_map/ppermute | solution.py:220
  53.6 9.6 %collective-permute-start.5 = (f32[256,256]{1,0:T(8,128)S(1)}, f32[256,256]{1,0:T(8,128)S(1)}, u32[]{:S(2)}, u32[]{:S(2)}) collective-permute-start(f32[256,256]{1,0:T(8,128)S(1)} %collective-permute-done.2.refs_1_), channel_id=1, source_target_pairs={{0,4},{1,5},{2,6},{3,7},{4,0},{5,1},{6,2},{7,3},{8,12},{9,13},{10,... | collective-permute-start | bytes 786440 | tf_op jit(solution)/shard_map/ppermute | solution.py:224
  57.7 6.9 %collective-permute-start.4 = (f32[256,256]{1,0:T(8,128)S(1)}, f32[256,256]{1,0:T(8,128)S(1)}, u32[]{:S(2)}, u32[]{:S(2)}) collective-permute-start(f32[256,256]{1,0:T(8,128)S(1)} %collective-permute-done.1.refs_0_), channel_id=1, source_target_pairs={{0,3},{1,0},{2,1},{3,2},{4,7},{5,4},{6,5},{7,6},{8,11},{9,8},{10,9... | collective-permute-start | bytes 786440 | tf_op jit(solution)/shard_map/ppermute | solution.py:227
  60.8 7.6 %collective-permute-start.3 = (f32[256,256]{1,0:T(8,128)S(1)}, f32[256,256]{1,0:T(8,128)S(1)}, u32[]{:S(2)}, u32[]{:S(2)}) collective-permute-start(f32[256,256]{1,0:T(8,128)S(1)} %collective-permute-done.1.refs_0_), channel_id=1, source_target_pairs={{0,1},{1,2},{2,3},{3,0},{4,5},{5,6},{6,7},{7,4},{8,9},{9,10},{10,1... | collective-permute-start | bytes 786440 | tf_op jit(solution)/shard_map/ppermute | solution.py:226
